TPU v7x, 256 devices: a whole 4x4x8 slice. The times are simulated.
256 devices in a mesh: group: 16 (over y, x), member: 16 (over z, core).
Axes of the slice: x: 4, y: 4, z: 8, core: 2. Of those that a mesh axis runs over, the one named last changes fastest.
Arguments:
- factor: float32 [16, 32, 768, 768], P('group', 'member'), as said below
- load: float32 [16, 32, 768], P('group', 'member'), may hold values from -6 to 6
- dof_map: int32 [16, 32, 768], P('group', 'member'), may hold values from 0 to 767, as said below
- dof_sign: int32 [16, 32, 768], P('group', 'member'), may hold values from -1 to 1, as said below
- live_count: int32 [16, 32], P('group', 'member'), may hold values from 384 to 768, as said below
- face_slot: int32 [16, 32, 4, 64], P('group', 'member'), may hold values from 0 to 767, as said below
- face_count: int32 [16, 32, 4], P('group', 'member'), may hold values from 0 to 64, as said below
- node_coord: int32 [16, 32, 3, 256], P('group', 'member'), may hold values from 0 to 15
- coarse_inverse: float32 [3072, 3072], P(('group', 'member')), as said below
Outputs:
- multipliers: float32 [16, 32, 768], P('group', 'member')
- projected: float32 [16, 32, 768], P('group', 'member')
Inputs may be any that keep to these rules, and one draw needn't show every extreme that they name: `dof_map`: each subdomain's row is a permutation of the unknowns. `dof_sign`: every entry is -1 or 1. `live_count`: in each cluster, both subdomains of one device have 768 live multipliers and both subdomains of the device whose member index differs by a quarter of 32 have 384. `face_slot`: the slots of one subdomain are distinct and below its live_count; slot k of a face pairs with slot k of the partner's face. `face_count`: A face and its partner's face have the same count; faces at the ends of a cluster's chain and at the first and last cluster have 0, all others 1 or more. `factor`: lower triangular with a positive diagonal. `coarse_inverse`: symmetric positive definite.
All inputs are finite; a program needn't handle non-finite values.
Results may differ from a plain program's by a relative error of at most 0.0003.
Values sent between devices are 32-bit elements; how exact they have to be, the bound alone decides.
No kernel may reach another device: no remote copies, remote signals or barrier semaphores. Data moves between devices by JAX's collectives and lax.ppermute only.
A program may use at most 128 MiB of HBM per device.

v0:
```python
import math

import jax
import jax.numpy as jnp
from jax import lax
from jax.sharding import PartitionSpec as P

ITERS = 3


highest = lax.Precision.HIGHEST
half_span = 8.0


def from_partner(value, axis, bit):
    mask = 2**bit
    pairs = [(source, source ^ mask) for source in range(lax.axis_size(axis))]
    return lax.ppermute(value, axis, pairs)


def padded(array, sides, width):
    for axis, dim in sides:
        size, length = (lax.axis_size(axis), array.shape[dim])
        up = [(i, (i + 1) % size) for i in range(size - 1)]
        down = [(j, i) for i, j in up]
        last = lax.slice_in_dim(array, length - width, length, axis=dim)
        leading = lax.slice_in_dim(array, 0, width, axis=dim)
        before = lax.ppermute(last, axis, up)
        after = lax.ppermute(leading, axis, down)
        array = jnp.concatenate([before, array, after], axis=dim)
    return array


def rigid_modes(node_coord):
    position = (node_coord.astype(jnp.float32) - half_span) / half_span
    spread = jnp.repeat(position, 3, axis=-1)
    component = jnp.arange(spread.shape[-1], dtype=jnp.int32) % 3
    first = (component == 0).astype(spread.dtype)
    second = (component == 1).astype(spread.dtype)
    third = (component == 2).astype(spread.dtype)
    coord_x = spread[..., 0, :]
    coord_y = spread[..., 1, :]
    coord_z = spread[..., 2, :]
    unit_row = jnp.ones_like(coord_x)
    return jnp.stack(
        [
            first * unit_row,
            second * unit_row,
            third * unit_row,
            third * coord_y - second * coord_z,
            first * coord_z - third * coord_x,
            second * coord_x - first * coord_y,
        ],
        axis=-2,
    )


def lower_solve(panel_matrix, right_side):
    return lax.linalg.triangular_solve(panel_matrix, right_side, left_side=True, lower=True)


def upper_solve(panel_matrix, right_side):
    return lax.linalg.triangular_solve(
        panel_matrix, right_side, left_side=True, lower=True, transpose_a=True
    )


def dual_of(panel_matrix, dof_codes, block_count, block_width):
    dof_count = panel_matrix.shape[0]
    slot_total = dof_codes.shape[0]
    levels = jnp.arange(dof_count, dtype=jnp.float32)[:, None]

    def solve_block(block_index, solved):
        columns = lax.dynamic_slice_in_dim(dof_codes, block_index * block_width, block_width)
        target = jnp.where(
            levels == jnp.abs(columns)[None, :] - 1.0, jnp.sign(columns)[None, :], 0.0
        )
        solved_piece = lower_solve(panel_matrix, target)
        return lax.dynamic_update_slice_in_dim(solved, solved_piece, block_index * block_width, 1)

    solved = lax.fori_loop(
        0, block_count, solve_block, jnp.zeros((dof_count, slot_total), jnp.float32)
    )

    def product_block(block_index, dual_sum):
        solved_piece = lax.dynamic_slice_in_dim(solved, block_index * block_width, block_width, 1)
        column = lax.dot_general(
            solved,
            solved_piece,
            (((0,), (0,)), ((), ())),
            precision=highest,
            preferred_element_type=jnp.float32,
        )
        return lax.dynamic_update_slice_in_dim(dual_sum, column, block_index * block_width, 1)

    return lax.fori_loop(
        0, block_count, product_block, jnp.zeros((slot_total, slot_total), jnp.float32)
    )


def shards(
    factor, load, dof_map, dof_sign, live_count, face_slot, face_count, node_coord, coarse_inverse
):
    own_panels = factor[0]
    own_loads = load[0]
    dof_count = own_loads.shape[1]
    subs_here = own_loads.shape[0]
    face_cap = face_slot.shape[3]
    block_width = math.gcd(dof_count, 128)
    positions = jnp.arange(dof_count, dtype=jnp.int32)
    live_mask = positions[None, :] < live_count[0][:, None]
    signed = jnp.where(live_mask, dof_sign[0], 0)
    dof_codes = ((dof_map[0] + 1) * signed).astype(jnp.float32)
    signed_float = signed.astype(jnp.float32)
    blocks_own = (live_count[0] + block_width - 1) // block_width
    bit_pos = lax.axis_size("member").bit_length() - 2
    partner_panel, partner_codes = from_partner((own_panels[1], dof_codes), "member", bit_pos)
    first_dual = dual_of(own_panels[0], dof_codes[0], blocks_own[0], block_width)
    partner_blocks = (
        jnp.sum((partner_codes != 0).astype(jnp.int32), axis=1) + block_width - 1
    ) // block_width
    upper_half = lax.axis_index("member") // (lax.axis_size("member") // 2) % 2 == 1
    lower_blocks = jnp.where(upper_half, partner_blocks, blocks_own)
    upper_blocks = jnp.where(upper_half, blocks_own, partner_blocks)
    lower_loads = jnp.stack(
        [
            lower_blocks[0] + lower_blocks[1],
            lower_blocks[0],
            lower_blocks[0] + lower_blocks[1] + upper_blocks[1],
            lower_blocks[0] + upper_blocks[1],
        ]
    )
    upper_loads = jnp.stack(
        [
            upper_blocks[0] + upper_blocks[1],
            upper_blocks[0] + upper_blocks[1] + lower_blocks[1],
            upper_blocks[0],
            upper_blocks[0] + lower_blocks[1],
        ]
    )
    option_pick = jnp.argmin(jnp.maximum(lower_loads, upper_loads))
    lower_moves = (option_pick == 1) | (option_pick == 3)
    upper_moves = (option_pick == 2) | (option_pick == 3)
    give_mine = jnp.where(upper_half, upper_moves, lower_moves)
    take_theirs = jnp.where(upper_half, lower_moves, upper_moves)
    kept_dual = dual_of(
        own_panels[1], dof_codes[1], jnp.where(give_mine, 0, blocks_own[1]), block_width
    )
    helped_dual = dual_of(
        partner_panel, partner_codes[1], jnp.where(take_theirs, partner_blocks[1], 0), block_width
    )
    returned = from_partner(helped_dual, "member", bit_pos)
    second_dual = jnp.where(give_mine, returned, kept_dual)
    dual_pair = jnp.stack([first_dual, second_dual])
    forward = jax.vmap(lambda panel_one, load_one: lower_solve(panel_one, load_one[:, None]))(
        own_panels, own_loads
    )
    displaced = jax.vmap(upper_solve)(own_panels, forward)[:, :, 0]
    gap_local = jnp.take_along_axis(displaced, dof_map[0], axis=1) * signed_float
    mode_table = rigid_modes(node_coord[0])
    rigid_rows = jnp.take_along_axis(
        mode_table, jnp.broadcast_to(dof_map[0][:, None, :], mode_table.shape), axis=2
    )
    rigid_rows = rigid_rows * signed_float[:, None, :]
    coarse_rhs = jnp.einsum("lai,li->la", mode_table, own_loads, precision=highest)
    slot_list = face_slot[0].reshape(subs_here, 4 * face_cap)
    slot_used = (
        jnp.arange(face_cap, dtype=jnp.int32)[None, None, :] < face_count[0][:, :, None]
    ).reshape(subs_here, 4 * face_cap)
    slot_table = (
        (slot_list[:, :, None] == positions[None, None, :]) & slot_used[:, :, None]
    ).astype(jnp.float32)
    shared = jnp.sum(slot_table, axis=1)
    weight = live_mask.astype(jnp.float32) * (1.0 - 0.5 * shared)

    def assemble(values):
        outgoing = jnp.einsum("lkj,lj->lk", slot_table, values, precision=highest)
        extended = padded(outgoing[None], (("group", 0), ("member", 1)), 1)
        incoming = jnp.stack(
            [
                jnp.concatenate(
                    [
                        extended[1, sub_index, face_cap : 2 * face_cap],
                        extended[1, sub_index + 2, 0:face_cap],
                        extended[0, sub_index + 1, 3 * face_cap : 4 * face_cap],
                        extended[2, sub_index + 1, 2 * face_cap : 3 * face_cap],
                    ]
                )
                for sub_index in range(subs_here)
            ]
        )
        return values + jnp.einsum("lk,lkj->lj", incoming, slot_table, precision=highest)

    def inner_part(left_field, right_field):
        return jnp.sum(weight * left_field * right_field)

    def global_sum(partial_value):
        return lax.psum(partial_value, ("group", "member"))

    def gather_coarse(local_coarse):
        return lax.all_gather(local_coarse.reshape(1, -1), ("group", "member"), axis=0, tiled=True)

    def coarse_of(values):
        return jnp.einsum("laj,lj->la", rigid_rows, values, precision=highest)

    def spread_modes(gathered):
        alpha = jnp.dot(coarse_inverse, gathered.reshape(-1), precision=highest).reshape(
            subs_here, -1
        )
        return assemble(jnp.einsum("laj,la->lj", rigid_rows, alpha, precision=highest))

    def apply_dual(values):
        return jnp.einsum("lij,lj->li", dual_pair, values, precision=highest)

    multipliers = spread_modes(gather_coarse(coarse_rhs))
    residual = assemble(gap_local - apply_dual(multipliers))
    coarse_res = gather_coarse(coarse_of(residual))
    projected = residual - spread_modes(coarse_res)
    direction = projected
    norm_now = global_sum(inner_part(projected, projected))
    for iteration in range(ITERS):
        image_vec = assemble(apply_dual(direction))
        curvature = global_sum(inner_part(direction, image_vec))
        step_size = norm_now / curvature
        multipliers = multipliers + step_size * direction
        residual = residual - step_size * image_vec
        coarse_res = gather_coarse(coarse_of(residual))
        projected = residual - spread_modes(coarse_res)
        norm_next = global_sum(inner_part(projected, projected))
        direction = projected + norm_next / norm_now * direction
        norm_now = norm_next
    return (multipliers[None], projected[None])


def solution(mesh):
    return jax.shard_map(
        shards,
        mesh=mesh,
        in_specs=(
            P("group", "member", None, None),
            P("group", "member", None),
            P("group", "member", None),
            P("group", "member", None),
            P("group", "member"),
            P("group", "member", None, None),
            P("group", "member", None),
            P("group", "member", None, None),
            P(("group", "member"), None),
        ),
        out_specs=(P("group", "member", None), P("group", "member", None)),
        check_vma=False,
    )
```

profile of v0, /device:TPU:1, one launch (start us, length us, event | category | flops | bytes accessed | tf_op | source)
XLA Modules:
  0.0 2191.7 jit_solution(2142416162315321795)
XLA Ops:
  4.6 71.1 %gather_fusion = f32[9216]{0:T(1024)S(1)} fusion(f32[2,6,768]{2,1,0:T(8,128)S(1)} %stack.144, s32[9216]{0:T(1024)S(1)} %reshape.418), kind=kCustom, calls=%fused_computation | custom fusion | bytes 184320 | tf_op jit(solution)/shard_map/jit(take_along_axis)/gather | solution.py:161
  75.9 61.2 %all-gather = f32[256,1,12]{2,1,0:T(1,128)S(1)} all-gather(f32[1,1,12]{2,1,0:T(1,128)S(1)} %reshape.430), channel_id=1, replica_groups=mesh['group'=16,'member'=16] {'group','member'}, dimensions={0}, use_global_device_ids=true | all-gather | bytes 12336 | tf_op jit(solution)/shard_map/all_gather | solution.py:201
  162.2 18.4 while.82
  180.6 117.9 %custom-call.8 = f32[2,6,128,128]{2,3,1,0:T(8,128)S(1)} custom-call(f32[2,6,128,128]{3,2,1,0:T(8,128)S(1)} %bitcast.1018), custom_call_target="InvertDiagBlocksLowerTriangular" | custom-call | tf_op jit(solution)/shard_map/vmap()/triangular_solve | solution.py:63
  352.6 324.7 %while.88 = (s32[]{:T(128)}, f32[768,768]{1,0:T(8,128)}, s32[]{:T(128)}, f32[768]{0:T(1024)S(1)}, f32[768,768]{1,0:T(8,128)}, /*index=5*/s32[]{:T(128)}, s32[]{:T(128)}, s32[]{:T(128)}, s32[]{:T(128)}, s32[]{:T(128)}) while((s32[]{:T(128)}, f32[768,768]{1,0:T(8,128)}, s32[]{:T(128)}, f32[768]{0:T(1024)S(1)}, ...), condition=%wide.region_12.14_spmd.clone, body=%wide.region_11.13_spmd.clone.sunk | while | flops 530268544 | bytes 10424716 | solution.py:81
  354.9 15.0 while.91
  369.9 59.8 %custom-call.57 = f32[6,128,128]{1,2,0:T(8,128)S(1)} custom-call(f32[6,128,128]{2,1,0:T(8,128)} %get-tuple-element.1070), custom_call_target="InvertDiagBlocksLowerTriangular" | custom-call | tf_op jit(solution)/shard_map/while/body/triangular_solve/custom-call.1 | solution.py:59
  451.0 59.8 %custom-call.57 = f32[6,128,128]{1,2,0:T(8,128)S(1)} custom-call(f32[6,128,128]{2,1,0:T(8,128)} %get-tuple-element.1070), custom_call_target="InvertDiagBlocksLowerTriangular" | custom-call | tf_op jit(solution)/shard_map/while/body/triangular_solve/custom-call.1 | solution.py:59
  517.1 15.0 while.91
  532.2 59.8 %custom-call.57 = f32[6,128,128]{1,2,0:T(8,128)S(1)} custom-call(f32[6,128,128]{2,1,0:T(8,128)} %get-tuple-element.1070), custom_call_target="InvertDiagBlocksLowerTriangular" | custom-call | tf_op jit(solution)/shard_map/while/body/triangular_solve/custom-call.1 | solution.py:59
  613.3 59.8 %custom-call.57 = f32[6,128,128]{1,2,0:T(8,128)S(1)} custom-call(f32[6,128,128]{2,1,0:T(8,128)} %get-tuple-element.1070), custom_call_target="InvertDiagBlocksLowerTriangular" | custom-call | tf_op jit(solution)/shard_map/while/body/triangular_solve/custom-call.1 | solution.py:59
  686.8 330.9 %while.84 = (s32[]{:T(128)}, f32[768,768]{1,0:T(8,128)}, s32[]{:T(128)}, f32[768]{0:T(1024)S(1)}, f32[768,768]{1,0:T(8,128)}, /*index=5*/s32[]{:T(128)}, s32[]{:T(128)}, s32[]{:T(128)}, s32[]{:T(128)}, s32[]{:T(128)}) while((s32[]{:T(128)}, f32[768,768]{1,0:T(8,128)}, s32[]{:T(128)}, f32[768]{0:T(1024)S(1)}, f32[768,768]{1,0:T(8,128)}, ...), condition=%wide.region_2.4_spmd.clone, body=%wide.region_1.3_spmd.clone.sunk | while | flops 530268544 | bytes 10424716 | solution.py:81
  689.5 15.9 while.89
  705.3 59.8 %custom-call.51 = f32[6,128,128]{1,2,0:T(8,128)S(1)} custom-call(f32[6,128,128]{2,1,0:T(8,128)} %get-tuple-element.1024), custom_call_target="InvertDiagBlocksLowerTriangular" | custom-call | tf_op jit(solution)/shard_map/while/body/triangular_solve/custom-call.1 | solution.py:59
  772.0 15.9 while.89
  787.9 59.8 %custom-call.51 = f32[6,128,128]{1,2,0:T(8,128)S(1)} custom-call(f32[6,128,128]{2,1,0:T(8,128)} %get-tuple-element.1024), custom_call_target="InvertDiagBlocksLowerTriangular" | custom-call | tf_op jit(solution)/shard_map/while/body/triangular_solve/custom-call.1 | solution.py:59
  854.6 15.9 while.89
  870.5 59.8 %custom-call.51 = f32[6,128,128]{1,2,0:T(8,128)S(1)} custom-call(f32[6,128,128]{2,1,0:T(8,128)} %get-tuple-element.1024), custom_call_target="InvertDiagBlocksLowerTriangular" | custom-call | tf_op jit(solution)/shard_map/while/body/triangular_solve/custom-call.1 | solution.py:59
  937.2 15.9 while.89
  953.1 59.8 %custom-call.51 = f32[6,128,128]{1,2,0:T(8,128)S(1)} custom-call(f32[6,128,128]{2,1,0:T(8,128)} %get-tuple-element.1024), custom_call_target="InvertDiagBlocksLowerTriangular" | custom-call | tf_op jit(solution)/shard_map/while/body/triangular_solve/custom-call.1 | solution.py:59
  1032.7 16.6 while.79
  1056.5 90.8 %collective-permute-start.7 = (f32[1,2,256]{2,1,0:T(2,128)S(1)}, f32[1,2,256]{2,1,0:T(2,128)S(1)}, u32[]{:S(2)}, u32[]{:S(2)}) collective-permute-start(f32[1,2,256]{2,1,0:T(2,128)S(1)} %bitcast.930), channel_id=1, source_target_pairs={{0,16},{16,32},{32,48},{48,64},{64,80},{80,96},{96,112},{112,128},... | collective-permute-start | bytes 6152 | tf_op jit(solution)/shard_map/ppermute | solution.py:28
  1151.7 260.5 %collective-permute-start.9 = (f32[3,1,256]{2,1,0:T(1,128)S(1)}, f32[3,1,256]{2,1,0:T(1,128)S(1)}, u32[]{:S(2)}, u32[]{:S(2)}) collective-permute-start(f32[3,1,256]{2,1,0:T(1,128)S(1)} %get-tuple-element.616), channel_id=1, source_target_pairs={{0,1},{1,2},{2,3},{3,4},{4,5},{5,6},{6,7},{7,8},{8,9},{9,10},{10,1... | collective-permute-start | bytes 9224 | tf_op jit(solution)/shard_map/ppermute | solution.py:28
  1418.2 59.5 %all-gather.1 = f32[256,1,12]{2,1,0:T(1,128)S(1)} all-gather(f32[1,1,12]{2,1,0:T(1,128)S(1)} %reshape.432), channel_id=1, replica_groups=mesh['group'=16,'member'=16] {'group','member'}, dimensions={0}, use_global_device_ids=true | all-gather | bytes 12336 | tf_op jit(solution)/shard_map/all_gather | solution.py:201
  1520.8 79.5 %all-reduce = (f32[]{:T(128)}, f32[]{:T(128)}) all-reduce(f32[]{:T(128)} %get-tuple-element.439, f32[]{:T(128)} %get-tuple-element.438), channel_id=1, replica_groups=mesh['group'=16,'member'=16] {'group','member'}, use_global_device_ids=true, to_apply=%region_16.18 | all-reduce | flops 2 | bytes 16 | tf_op jit(solution)/shard_map/psum | solution.py:198
  1601.9 53.9 %all-gather.2 = f32[256,1,12]{2,1,0:T(1,128)S(1)} all-gather(f32[1,1,12]{2,1,0:T(1,128)S(1)} %reshape.434), channel_id=1, replica_groups=mesh['group'=16,'member'=16] {'group','member'}, dimensions={0}, use_global_device_ids=true | all-gather | bytes 12336 | tf_op jit(solution)/shard_map/all_gather | solution.py:201
  1677.4 77.4 %psum.44 = f32[]{:T(128)} all-reduce(f32[]{:T(128)} %fusion.217), channel_id=1, replica_groups=mesh['group'=16,'member'=16] {'group','member'}, use_global_device_ids=true, to_apply=%region_20.22 | all-reduce | flops 1 | bytes 8 | tf_op jit(solution)/shard_map/psum | solution.py:198
  1778.5 78.7 %psum.45 = f32[]{:T(128)} all-reduce(f32[]{:T(128)} %multiply_reduce_fusion.1), channel_id=1, replica_groups=mesh['group'=16,'member'=16] {'group','member'}, use_global_device_ids=true, to_apply=%region_22.24 | all-reduce | flops 1 | bytes 8 | tf_op jit(solution)/shard_map/psum | solution.py:198
  1858.9 54.1 %all-gather.3 = f32[256,1,12]{2,1,0:T(1,128)S(1)} all-gather(f32[1,1,12]{2,1,0:T(1,128)S(1)} %reshape.436), channel_id=1, replica_groups=mesh['group'=16,'member'=16] {'group','member'}, dimensions={0}, use_global_device_ids=true | all-gather | bytes 12336 | tf_op jit(solution)/shard_map/all_gather | solution.py:201
  1934.5 77.4 %psum.46 = f32[]{:T(128)} all-reduce(f32[]{:T(128)} %get-tuple-element.530), channel_id=1, replica_groups=mesh['group'=16,'member'=16] {'group','member'}, use_global_device_ids=true, to_apply=%region_24.26 | all-reduce | flops 1 | bytes 8 | tf_op jit(solution)/shard_map/psum | solution.py:198
  2035.5 78.9 %psum.47 = f32[]{:T(128)} all-reduce(f32[]{:T(128)} %multiply_reduce_fusion), channel_id=1, replica_groups=mesh['group'=16,'member'=16] {'group','member'}, use_global_device_ids=true, to_apply=%region_26.28 | all-reduce | flops 1 | bytes 8 | tf_op jit(solution)/shard_map/psum | solution.py:198
  2116.1 53.9 %all-gather.4 = f32[256,1,12]{2,1,0:T(1,128)S(1)} all-gather(f32[1,1,12]{2,1,0:T(1,128)S(1)} %reshape.438), channel_id=1, replica_groups=mesh['group'=16,'member'=16] {'group','member'}, dimensions={0}, use_global_device_ids=true | all-gather | bytes 12336 | tf_op jit(solution)/shard_map/all_gather | solution.py:201
  (695 shorter events, 515.5 us)
Async XLA Ops:
  141.7 188.2 %collective-permute-start = (f32[1,2,256]{2,1,0:T(2,128)S(1)}, f32[1,2,256]{2,1,0:T(2,128)S(1)}, u32[]{:S(2)}, u32[]{:S(2)}) collective-permute-start(f32[1,2,256]{2,1,0:T(2,128)S(1)} %bitcast.922), channel_id=1, source_target_pairs={{0,16},{16,32},{32,48},{48,64},{64,80},{80,96},{96,112},{112,128},... | collective-permute-start | bytes 6152 | tf_op jit(solution)/shard_map/ppermute | solution.py:28
  144.5 185.4 %collective-permute-start.1 = (f32[1,2,256]{2,1,0:T(2,128)S(1)}, f32[1,2,256]{2,1,0:T(2,128)S(1)}, u32[]{:S(2)}, u32[]{:S(2)}) collective-permute-start(f32[1,2,256]{2,1,0:T(2,128)S(1)} %bitcast.923), channel_id=1, source_target_pairs={{16,0},{32,16},{48,32},{64,48},{80,64},{96,80},{112,96},{128,112},... | collective-permute-start | bytes 6152 | tf_op jit(solution)/shard_map/ppermute | solution.py:29
  145.8 192.8 %collective-permute-start.4 = (f32[2,768]{1,0:T(2,128)S(1)}, f32[2,768]{1,0:T(2,128)S(1)}, u32[]{:S(2)}, u32[]{:S(2)}) collective-permute-start(f32[2,768]{1,0:T(2,128)S(1)} %get-tuple-element.600), channel_id=1, source_target_pairs={{0,8},{1,9},{2,10},{3,11},{4,12},{5,13},{6,14},{7,15},{8,0},{9,1},... | collective-permute-start | bytes 18440 | tf_op jit(solution)/shard_map/ppermute | solution.py:18
  153.2 525.4 %collective-permute-start.5 = (f32[768,768]{1,0:T(8,128)}, f32[768,768]{1,0:T(8,128)}, u32[]{:S(2)}, u32[]{:S(2)}) collective-permute-start(f32[768,768]{1,0:T(8,128)} %get-tuple-element.1222), channel_id=1, source_target_pairs={{0,8},{1,9},{2,10},{3,11},{4,12},{5,13},{6,14},{7,15},{8,0},{9,1},... | collective-permute-start | bytes 7077896 | tf_op jit(solution)/shard_map/ppermute | solution.py:18
  330.0 4.9 collective-permute-start.2
  332.8 4.9 collective-permute-start.3
  681.9 367.4 %collective-permute-start.6 = (f32[768,768]{0,1:T(8,128)}, f32[768,768]{0,1:T(8,128)}, u32[]{:S(2)}, u32[]{:S(2)}) collective-permute-start(f32[768,768]{0,1:T(8,128)} %get-tuple-element.317), channel_id=1, source_target_pairs={{0,8},{1,9},{2,10},{3,11},{4,12},{5,13},{6,14},{7,15},{8,0},{9,1},... | collective-permute-start | bytes 7077896 | tf_op jit(solution)/shard_map/ppermute | solution.py:18
  1056.5 92.1 %collective-permute-start.7 = (f32[1,2,256]{2,1,0:T(2,128)S(1)}, f32[1,2,256]{2,1,0:T(2,128)S(1)}, u32[]{:S(2)}, u32[]{:S(2)}) collective-permute-start(f32[1,2,256]{2,1,0:T(2,128)S(1)} %bitcast.930), channel_id=1, source_target_pairs={{0,16},{16,32},{32,48},{48,64},{64,80},{80,96},{96,112},{112,128},... | collective-permute-start | bytes 6152 | tf_op jit(solution)/shard_map/ppermute | solution.py:28
  1147.3 4.3 collective-permute-start.8
  1151.7 262.5 %collective-permute-start.9 = (f32[3,1,256]{2,1,0:T(1,128)S(1)}, f32[3,1,256]{2,1,0:T(1,128)S(1)}, u32[]{:S(2)}, u32[]{:S(2)}) collective-permute-start(f32[3,1,256]{2,1,0:T(1,128)S(1)} %get-tuple-element.616), channel_id=1, source_target_pairs={{0,1},{1,2},{2,3},{3,4},{4,5},{5,6},{6,7},{7,8},{8,9},{9,10},{10,1... | collective-permute-start | bytes 9224 | tf_op jit(solution)/shard_map/ppermute | solution.py:28
  1412.2 4.9 collective-permute-start.10
  1481.3 4.5 collective-permute-start.11
  1488.7 5.4 collective-permute-start.13
  1492.2 4.9 collective-permute-start.14
  1503.0 5.0 collective-permute-start.15
  1511.0 5.4 collective-permute-start.17
  1514.4 4.9 collective-permute-start.18
  1659.5 5.0 collective-permute-start.19
  1667.4 5.6 collective-permute-start.21
  1671.0 4.9 collective-permute-start.22
  1761.2 4.5 collective-permute-start.23
  1768.7 5.5 collective-permute-start.25
  1772.2 4.9 collective-permute-start.26
  1916.6 5.1 collective-permute-start.27
  1924.7 5.5 collective-permute-start.29
  1928.2 4.9 collective-permute-start.30
  2018.4 4.5 collective-permute-start.31
  2025.9 5.4 collective-permute-start.33
  2029.2 4.9 collective-permute-start.34
  2173.6 5.7 collective-permute-start.35
  2181.6 5.5 collective-permute-start.37
  2185.2 4.9 collective-permute-start.38
  (16 other events, 669.7 us)
where the time goes:
time: 2200 us; the launch traced here: 2190 us
  blocking collectives  675 us (31%)
  other arithmetic  636 us (29%)
  starting transfers between devices  443 us (20%)
  local copies, waits for them, and re-layouts  255 us (12%)
  matrix products  109 us (5%)
  waiting for transfers between devices  47.8 us (2%)
    another operation x40, other arithmetic, lower_solve(): lax.linalg.triangular_solve(panel_matrix, right_side, left_side=True, low...  493 us
    ppermute x18, starting transfers between devices, padded(): before = lax.ppermute(last, axis, up)  405 us
    psum x5, blocking collectives, global_sum(): return lax.psum(partial_value, ('group', 'member'))  392 us
    all_gather x5, blocking collectives, gather_coarse(): lax.all_gather(local_coarse.reshape(1, -1), ('group', 'member'), axis=0,...  283 us
    another operation x154, local copies, waits for them, and re-layouts, lower_solve(): lax.linalg.triangular_solve(panel_matrix, right_side, left_side=True, low...  123 us
    another operation x12, other arithmetic, upper_solve(): lax.linalg.triangular_solve(panel_matrix, right_side, left_side=True, low...  123 us
    gather x3, local copies, waits for them, and re-layouts, shards(): jnp.take_along_axis(mode_table, jnp.broadcast_to(dof_map[0][:, None, :],...  71.1 us
    ppermute x18, waiting for transfers between devices, padded(): after = lax.ppermute(leading, axis, down)  47.8 us
  transfers between devices with their start and end apart: 39, of which 17 were waited for; matrix products, arithmetic and copies ran while one was open for 40% of the time, Pallas kernels for 0%

commit v1 on v0

v1 whole, which is shorter than its diff:
```python
import jax
import jax.numpy as jnp
from jax import lax
from jax.experimental import pallas as pl
from jax.experimental.pallas import tpu as pltpu
from jax.sharding import PartitionSpec as P

ITERS = 3
ND = 768
LN = 128
NCH = ND // LN
DEV = 256
F32 = jnp.float32
BF = jnp.bfloat16
HI = lax.Precision.HIGHEST
NT = (((1,), (1,)), ((), ()))


def iota(shape, dim):
    return lax.broadcasted_iota(jnp.int32, shape, dim)


def tables_kernel(
    load_ref, map_ref, sign_ref, live_ref, slot_ref, used_ref, node_ref,
    tt_ref, qt_ref, rface_ref, own_ref, aux_ref, pay_ref,
):
    lane8 = iota((8, LN), 1)
    sub8 = iota((8, LN), 0)
    row = jnp.zeros((1, LN), F32)
    dim = iota((1, ND), 1).astype(F32)
    node = jnp.floor((dim + 0.5) * (1.0 / 3.0))
    comp = dim - 3.0 * node
    first = (comp == 0.0).astype(F32)
    second = (comp == 1.0).astype(F32)
    third = (comp == 2.0).astype(F32)
    delta = iota((256, ND), 1) - 3 * iota((256, ND), 0)
    rep = jnp.where((delta >= 0) & (delta < 3), 1.0, 0.0).astype(BF)
    for s in range(2):
        live = iota((1, ND), 1) < live_ref[s]
        live_f = jnp.where(live, 1.0, 0.0)
        sgn = jnp.where(live, sign_ref[s : s + 1, :].astype(F32), 0.0)
        dof = map_ref[s : s + 1, :]
        dof_f = dof.astype(F32)
        high = jnp.floor(dof_f * (1.0 / 32.0))
        low = dof_f - 32.0 * high
        part = iota((8, ND), 0)
        lhs = jnp.where(part == 0, high, jnp.where(part == 1, low, jnp.where(part == 2, sgn, 0.0)))
        slots = slot_ref[s : s + 1, :]
        used = used_ref[s : s + 1, :] > 0
        hit = jnp.where((iota((ND, 256), 0) == slots) & used, 1.0, 0.0).astype(BF)
        got = jnp.dot(lhs.astype(BF), hit, preferred_element_type=F32)
        dk = (32.0 * got[0:1, :] + got[1:2, :]).astype(jnp.int32)
        sk = got[2:3, :]
        tt = jnp.where(iota((ND, 256), 0) == dk, sk, 0.0)
        tt_b = tt.astype(BF)
        tt_ref[s] = tt_b
        qt = jnp.where(iota((ND, ND), 0) == dof, 1.0, 0.0).astype(BF)
        qt_ref[s] = qt
        mask = lax.dot_general(
            jnp.broadcast_to(live_f, (8, ND)).astype(BF), qt, NT, preferred_element_type=F32
        )[0:1, :]
        count = lax.dot_general(
            jnp.ones((8, 256), BF), jnp.abs(tt).astype(BF), NT, preferred_element_type=F32
        )[0:1, :]
        aux_ref[s : s + 1, :] = mask
        aux_ref[2 + s : 3 + s, :] = mask * (1.0 - 0.5 * count)
        aux_ref[4 + s : 5 + s, :] = sgn
        aux_ref[6 + s : 7 + s, :] = jnp.zeros((1, ND), F32)
        position = (node_ref[s].astype(F32) - 8.0) * 0.125
        spread = jnp.dot(position.astype(BF), rep, preferred_element_type=F32)
        cx = spread[0:1, :]
        cy = spread[1:2, :]
        cz = spread[2:3, :]
        rows = (
            first, second, third,
            third * cy - second * cz,
            first * cz - third * cx,
            second * cx - first * cy,
        )
        modes = jnp.zeros((8, ND), F32)
        for a in range(6):
            modes = jnp.where(part == a, rows[a], modes)
        own_ref[s] = modes * mask
        rface_ref[s] = jnp.dot(modes.astype(BF), tt_b, preferred_element_type=F32)
        e = jnp.sum(modes * load_ref[s : s + 1, :], axis=1, keepdims=True)
        row = row + jnp.sum(jnp.where(lane8 == sub8 + 8 * s, e, 0.0), axis=0, keepdims=True)
    pay_ref[...] = jnp.broadcast_to(row, (DEV, LN))


def half_masks(rows):
    return iota((rows, LN), 1) < 64


def pack_faces(o0, o1):
    lo = half_masks(o0.shape[0])
    o0l, o0h, o1l, o1h = o0[:, :LN], o0[:, LN:], o1[:, :LN], o1[:, LN:]
    to_gm = jnp.where(lo, o0h, pltpu.roll(o1h, 64, 1))
    to_gp = jnp.where(lo, pltpu.roll(o0h, 64, 1), o1h)
    return o0l, o1l, to_gm, to_gp


def spread_kernel(rf_ref, nb_ref, own_ref, tt_ref, ar_ref):
    lo = half_masks(8)
    zero = jnp.zeros((8, LN), F32)
    left, right, gm, gp = nb_ref[0], nb_ref[1], nb_ref[2], nb_ref[3]
    r0l, r1l = rf_ref[0][:, :LN], rf_ref[1][:, :LN]

    def both(a, b):
        return jnp.concatenate([a, b], axis=1)

    w0 = [
        both(zero, zero),
        both(pltpu.roll(jnp.where(lo, r1l, 0.0), 64, 1), zero),
        both(pltpu.roll(jnp.where(lo, 0.0, left), 64, 1), zero),
        both(zero, jnp.where(lo, gm, 0.0)),
        both(zero, jnp.where(lo, 0.0, pltpu.roll(gp, 64, 1))),
    ]
    w1 = [
        both(pltpu.roll(jnp.where(lo, 0.0, r0l), 64, 1), zero),
        both(zero, zero),
        both(pltpu.roll(jnp.where(lo, right, 0.0), 64, 1), zero),
        both(zero, jnp.where(lo, pltpu.roll(gm, 64, 1), 0.0)),
        both(zero, jnp.where(lo, 0.0, gp)),
    ]
    for s, w in ((0, w0), (1, w1)):
        table = jnp.concatenate(w, axis=0).astype(BF)
        ar_ref[s] = lax.dot_general(table, tt_ref[s], NT, preferred_element_type=F32)
        at = 8 * s
        ar_ref[s, at : at + 8, :] = own_ref[s]


def mm(a, b):
    return jnp.dot(a, b, precision=HI, preferred_element_type=F32)


def invert_kernel(l_ref, out_ref, n_ref, x_ref):
    ri = iota((LN, LN), 0)
    ci = iota((LN, LN), 1)
    eye = ri == ci
    below = ri > ci

    def block(s, i, j, width=LN):
        return l_ref[s, i * width : (i + 1) * width, j * width : (j + 1) * width]

    nblocks = 2 * NCH
    for k in range(nblocks):
        s, b = divmod(k, NCH)
        lb = block(s, b, b)
        diag = jnp.sum(jnp.where(eye, lb, 0.0), axis=1, keepdims=True)
        n = jnp.where(below, lb * (1.0 / diag), 0.0)
        n_ref[k] = n
        x_ref[k] = jnp.where(eye, 1.0, 0.0) - jnp.where((ri // 2) == (ci // 2), n, 0.0)
    size = 2
    while size < LN:
        pick = ((ri // (2 * size)) == (ci // (2 * size))) & ((ri // size) != (ci // size))
        inner = [mm(jnp.where(pick, n_ref[k], 0.0), x_ref[k]) for k in range(nblocks)]
        for k in range(nblocks):
            x = x_ref[k]
            x_ref[k] = x - mm(x, inner[k])
        size *= 2
    for k in range(nblocks):
        s, b = divmod(k, NCH)
        diag = jnp.sum(jnp.where(eye, block(s, b, b), 0.0), axis=0, keepdims=True)
        x_ref[k] = x_ref[k] * (1.0 / diag)
    zero = jnp.zeros((LN, LN), F32)
    big = {}
    for s in range(2):
        for q in range(NCH // 2):
            upper = x_ref[s * NCH + 2 * q]
            lower = x_ref[s * NCH + 2 * q + 1]
            corner = -mm(lower, mm(block(s, 2 * q + 1, 2 * q), upper))
            at = 2 * q * LN
            out_ref[s, at : at + LN, at : at + LN] = upper
            out_ref[s, at : at + LN, at + LN : at + 2 * LN] = zero
            out_ref[s, at + LN : at + 2 * LN, at : at + LN] = corner
            out_ref[s, at + LN : at + 2 * LN, at + LN : at + 2 * LN] = lower
    wd = 2 * LN

    def inv(s, i, j):
        return out_ref[s, i * wd : (i + 1) * wd, j * wd : (j + 1) * wd]

    for s in range(2):
        out_ref[s, wd : 2 * wd, 0:wd] = -mm(inv(s, 1, 1), mm(block(s, 1, 0, wd), inv(s, 0, 0)))
    for s in range(2):
        out_ref[s, 2 * wd : 3 * wd, wd : 2 * wd] = -mm(
            inv(s, 2, 2), mm(block(s, 2, 1, wd), inv(s, 1, 1))
        )
    for s in range(2):
        mid = mm(block(s, 2, 0, wd), inv(s, 0, 0)) + mm(block(s, 2, 1, wd), inv(s, 1, 0))
        out_ref[s, 2 * wd : 3 * wd, 0:wd] = -mm(inv(s, 2, 2), mid)


def split3(rows, total):
    idx = iota((total, rows[0].shape[1]), 0)
    out = jnp.zeros((total, rows[0].shape[1]), F32)
    for r, z in enumerate(rows):
        h = z.astype(BF).astype(F32)
        rest = z - h
        m = rest.astype(BF).astype(F32)
        l = rest - m
        out = jnp.where(idx == 3 * r, h, out)
        out = jnp.where(idx == 3 * r + 1, m, out)
        out = jnp.where(idx == 3 * r + 2, l, out)
    return out.astype(BF)


def solve(inv_ref, s, z):
    ys = []
    for b in range(NCH):
        acc = None
        for c in range(b + 1):
            term = inv_ref[s, b * LN : (b + 1) * LN, c * LN : (c + 1) * LN] * z[:, c * LN : (c + 1) * LN]
            acc = term if acc is None else acc + term
        ys.append(jnp.sum(acc, axis=1, keepdims=True))
    us = []
    for c in range(NCH):
        acc = None
        for b in range(c, NCH):
            term = inv_ref[s, b * LN : (b + 1) * LN, c * LN : (c + 1) * LN] * ys[b]
            acc = term if acc is None else acc + term
        us.append(jnp.sum(acc, axis=0, keepdims=True))
    return jnp.concatenate(us, axis=1)


def received_coarse(recv_ref):
    xt = jnp.transpose(recv_ref[:, 0:LN])

    def grp(i):
        return xt[8 * i : 8 * i + 8, :]

    h0 = grp(0) + pltpu.roll(grp(2), 1, 1) + pltpu.roll(grp(4), DEV - 16, 1) + pltpu.roll(grp(6), 16, 1)
    h1 = grp(1) + pltpu.roll(grp(3), DEV - 1, 1) + pltpu.roll(grp(5), DEV - 16, 1) + pltpu.roll(grp(7), 16, 1)
    sums = jnp.sum(grp(8), axis=1, keepdims=True)
    return h0, h1, sums


def project_rows(h0, h1, m_ref, ar_ref):
    acc = jnp.zeros((64, DEV), F32)
    for v in range(12):
        h = h0 if v < 6 else h1
        a = v % 6
        acc = acc + m_ref[:, v * DEV : (v + 1) * DEV] * h[a : a + 1, :]
    al = jnp.sum(acc, axis=1, keepdims=True)

    def grp(i):
        return al[8 * i : 8 * i + 8, :]

    a0 = jnp.concatenate([grp(0), grp(1), grp(3), grp(4), grp(6)], axis=0)
    a1 = jnp.concatenate([grp(0), grp(1), grp(2), grp(5), grp(7)], axis=0)
    w0 = jnp.sum(ar_ref[0] * a0, axis=0, keepdims=True)
    w1 = jnp.sum(ar_ref[1] * a1, axis=0, keepdims=True)
    return w0, w1


def tile_of(row):
    base = pl.multiple_of((row // 8) * 8, 8)
    return base, row - base


def face_row(recv_ref, row):
    base, offset = tile_of(row)
    tile = recv_ref[pl.ds(base, 8), LN : 2 * LN]
    return jnp.sum(jnp.where(iota((8, LN), 0) == offset, tile, 0.0), axis=0, keepdims=True)


def assembled(pos_ref, recv_ref, y, o, tt_ref):
    lo = half_masks(1)
    left, right, gm, gp = (face_row(recv_ref, pos_ref[i]) for i in range(4))
    o0l, o1l = o[0][:, :LN], o[1][:, :LN]
    in0 = jnp.concatenate(
        [pltpu.roll(jnp.where(lo, o1l, left), 64, 1), jnp.where(lo, gm, pltpu.roll(gp, 64, 1))], axis=1
    )
    in1 = jnp.concatenate(
        [pltpu.roll(jnp.where(lo, right, o0l), 64, 1), jnp.where(lo, pltpu.roll(gm, 64, 1), gp)], axis=1
    )
    out = []
    for s, inc in ((0, in0), (1, in1)):
        add = lax.dot_general(split3([inc], 8), tt_ref[s], NT, preferred_element_type=F32)
        out.append(y[s] + jnp.sum(add, axis=0, keepdims=True))
    return out


def send(pos_ref, pay_ref, y, tt_ref, ar_ref, dots):
    o = []
    cols = []
    for s in range(2):
        prod = jnp.dot(split3([y[s]], 8), tt_ref[s], preferred_element_type=F32)
        o.append(jnp.sum(prod, axis=0, keepdims=True))
        cols.append(jnp.sum(ar_ref[s] * y[s], axis=1, keepdims=True))
    c0, c1 = cols

    def grp(c, i):
        return c[8 * i : 8 * i + 8, :]

    cc = jnp.concatenate(
        [
            grp(c0, 0) + grp(c1, 0), grp(c0, 1) + grp(c1, 1), grp(c1, 2), grp(c0, 2),
            grp(c0, 3), grp(c1, 3), grp(c0, 4), grp(c1, 4),
        ],
        axis=0,
    )
    diag = iota((64, LN), 0) == iota((64, LN), 1)
    row = jnp.sum(jnp.where(diag, cc, 0.0), axis=0, keepdims=True)
    lane = iota((1, LN), 1)
    for i, value in enumerate(dots):
        row = jnp.where(lane == 64 + i, value, row)
    pay_ref[:, 0:LN] = jnp.broadcast_to(row, (DEV, LN))
    pay_ref[:, LN : 2 * LN] = jnp.zeros((DEV, LN), F32)
    to_left, to_right, to_gm, to_gp = pack_faces(o[0], o[1])
    for i, face in enumerate((to_left, to_right, to_gm, to_gp)):
        base, offset = tile_of(pos_ref[i])
        old = pay_ref[pl.ds(base, 8), LN : 2 * LN]
        pay_ref[pl.ds(base, 8), LN : 2 * LN] = jnp.where(iota((8, LN), 0) == offset, face, old)
    return o


def inner(a, b):
    return jnp.sum(a[0] * b[0] + a[1] * b[1], axis=1, keepdims=True)


def pair(ref, i):
    return [ref[i : i + 1, :], ref[i + 1 : i + 2, :]]


def put(ref, i, v):
    ref[i : i + 1, :] = v[0]
    ref[i + 1 : i + 2, :] = v[1]


LAM, PV, DV, IM, YD, YV = 0, 2, 4, 6, 8, 10


def begin_kernel(pos_ref, recv_ref, load_ref, inv_ref, tt_ref, ar_ref, m_ref, aux_ref, st_ref, o_ref, pay_ref):
    h0, h1, _ = received_coarse(recv_ref)
    lam = project_rows(h0, h1, m_ref, ar_ref)
    mask = pair(aux_ref, 0)
    y = [mask[s] * solve(inv_ref, s, load_ref[s : s + 1, :] - lam[s]) for s in range(2)]
    o = send(pos_ref, pay_ref, y, tt_ref, ar_ref, [])
    put(st_ref, LAM, lam)
    put(st_ref, YV, y)
    put(o_ref, 0, o)


def next_solve(pos_ref, pay_ref, inv_ref, tt_ref, ar_ref, aux_ref, p, d, yd):
    mask = pair(aux_ref, 0)
    weight = pair(aux_ref, 2)
    y = [mask[s] * solve(inv_ref, s, p[s]) for s in range(2)]
    wp = [weight[s] * p[s] for s in range(2)]
    dots = [inner(wp, p), inner(p, y)]
    if d is not None:
        dots += [inner(d, y), inner(p, yd)]
    o = send(pos_ref, pay_ref, y, tt_ref, ar_ref, dots)
    return y, o


def first_kernel(pos_ref, recv_ref, st_ref, o_ref, inv_ref, tt_ref, ar_ref, m_ref, aux_ref, st2_ref, o2_ref, pay_ref):
    h0, h1, _ = received_coarse(recv_ref)
    w = project_rows(h0, h1, m_ref, ar_ref)
    res = assembled(pos_ref, recv_ref, pair(st_ref, YV), pair(o_ref, 0), tt_ref)
    p = [res[s] - w[s] for s in range(2)]
    y, o = next_solve(pos_ref, pay_ref, inv_ref, tt_ref, ar_ref, aux_ref, p, None, None)
    put(st2_ref, LAM, pair(st_ref, LAM))
    put(st2_ref, PV, p)
    put(st2_ref, YV, y)
    put(o2_ref, 0, o)


def step_body(it, pos_ref, recv_ref, st_ref, o_ref, hs_ref, tt_ref, ar_ref, m_ref):
    h0, h1, sums = received_coarse(recv_ref)
    norm = sums[0:1, :]
    y = pair(st_ref, YV)
    p = pair(st_ref, PV)
    image = assembled(pos_ref, recv_ref, y, pair(o_ref, 0), tt_ref)
    if it == 0:
        d, yd, curve = p, y, sums[1:2, :]
    else:
        beta = norm / hs_ref[16:17, 0:1]
        curve = sums[1:2, :] + beta * (sums[2:3, :] + sums[3:4, :]) + beta * beta * hs_ref[17:18, 0:1]
        dold, iold, yold = pair(st_ref, DV), pair(st_ref, IM), pair(st_ref, YD)
        d = [p[s] + beta * dold[s] for s in range(2)]
        yd = [y[s] + beta * yold[s] for s in range(2)]
        image = [image[s] + beta * iold[s] for s in range(2)]
        h0 = h0 + beta * hs_ref[0:8, :]
        h1 = h1 + beta * hs_ref[8:16, :]
    step = norm / curve
    w = project_rows(h0, h1, m_ref, ar_ref)
    lam = pair(st_ref, LAM)
    lam = [lam[s] + step * d[s] for s in range(2)]
    pn = [p[s] - step * (image[s] - w[s]) for s in range(2)]
    return lam, pn, d, yd, image, h0, h1, norm, curve


def make_step(it):
    def step_kernel(
        pos_ref, recv_ref, st_ref, o_ref, hs_ref, inv_ref, tt_ref, ar_ref, m_ref, aux_ref,
        st2_ref, o2_ref, hs2_ref, pay_ref,
    ):
        lam, pn, d, yd, image, h0, h1, norm, curve = step_body(
            it, pos_ref, recv_ref, st_ref, o_ref, hs_ref, tt_ref, ar_ref, m_ref
        )
        y, o = next_solve(pos_ref, pay_ref, inv_ref, tt_ref, ar_ref, aux_ref, pn, d, yd)
        for at, v in ((LAM, lam), (PV, pn), (DV, d), (IM, image), (YD, yd), (YV, y)):
            put(st2_ref, at, v)
        put(o2_ref, 0, o)
        hs2_ref[0:8, :] = h0
        hs2_ref[8:16, :] = h1
        hs2_ref[16:17, :] = jnp.broadcast_to(norm, (1, DEV))
        hs2_ref[17:18, :] = jnp.broadcast_to(curve, (1, DEV))

    return step_kernel


def last_kernel(pos_ref, recv_ref, st_ref, o_ref, hs_ref, tt_ref, ar_ref, m_ref, aux_ref, qt_ref, lam_ref, p_ref):
    lam, pn = step_body(ITERS - 1, pos_ref, recv_ref, st_ref, o_ref, hs_ref, tt_ref, ar_ref, m_ref)[:2]
    for s in range(2):
        got = jnp.dot(split3([lam[s], pn[s]], 8), qt_ref[s], preferred_element_type=F32)
        sgn = aux_ref[4 + s : 5 + s, :]
        lam_ref[s : s + 1, :] = sgn * jnp.sum(got[0:3, :], axis=0, keepdims=True)
        p_ref[s : s + 1, :] = sgn * jnp.sum(got[3:6, :], axis=0, keepdims=True)


def sds(shape, dtype=F32):
    return jax.ShapeDtypeStruct(shape, dtype)


VM = pl.BlockSpec(memory_space=pltpu.VMEM)
SM = pl.BlockSpec(memory_space=pltpu.SMEM)


def call(kernel, outs, smem, *args, scratch=(), flops=0, name=None):
    specs = [SM if i in smem else VM for i in range(len(args))]
    return pl.pallas_call(
        kernel,
        out_shape=outs,
        in_specs=specs,
        out_specs=tuple(VM for _ in outs),
        scratch_shapes=list(scratch),
        name=name,
        compiler_params=pltpu.CompilerParams(vmem_limit_bytes=40 * 2**20),
        cost_estimate=pl.CostEstimate(flops=flops, transcendentals=0, bytes_accessed=2**20)
        if flops
        else None,
    )(*args)


def shards(factor, load, dof_map, dof_sign, live_count, face_slot, face_count, node_coord, coarse_inverse):
    axes = ("group", "member")
    g = lax.axis_index("group")
    m = lax.axis_index("member")
    me = g * 16 + m
    pos = jnp.stack(
        [
            jnp.where(m > 0, me - 1, me),
            jnp.where(m < 15, me + 1, me),
            jnp.where(g > 0, me - 16, me),
            jnp.where(g < 15, me + 16, me),
        ]
    ).astype(jnp.int32)
    loads = load[0]
    slots = face_slot[0].reshape(2, 256)
    used = (jnp.arange(64, dtype=jnp.int32)[None, None, :] < face_count[0][:, :, None]).astype(jnp.int32)
    used = used.reshape(2, 256)
    tt, qt, rface, own, aux, pay0 = call(
        tables_kernel,
        (
            sds((2, ND, 256), BF), sds((2, ND, ND), BF), sds((2, 8, 256)), sds((2, 8, ND)),
            sds((8, ND)), sds((DEV, LN)),
        ),
        (3,),
        loads, dof_map[0], dof_sign[0], live_count[0], slots, used, node_coord[0],
        name="tables",
    )

    def exchange(pay):
        return lax.all_to_all(pay, axes, 0, 0, tiled=True)

    recv0 = exchange(pay0)
    rows = coarse_inverse.reshape(12, DEV, 12).transpose(0, 2, 1).reshape(2, 6, 12 * DEV)
    rows = jnp.pad(rows, ((0, 0), (0, 2), (0, 0)))
    up = [(i, i + 1) for i in range(15)]
    down = [(i + 1, i) for i in range(15)]
    lo = jnp.arange(LN) < 64
    r0h, r1h = rface[0][:, LN:], rface[1][:, LN:]
    to_gm = jnp.where(lo, r0h, jnp.roll(r1h, 64, 1))
    to_gp = jnp.where(lo, jnp.roll(r0h, 64, 1), r1h)
    from_right = lax.ppermute(jnp.concatenate([rows[0], rface[0][:, :LN]], axis=1), "member", down)
    from_left = lax.ppermute(jnp.concatenate([rows[1], rface[1][:, :LN]], axis=1), "member", up)
    flat = rows.reshape(16, 12 * DEV)
    pad8 = jnp.zeros((8, LN), F32)
    from_gp = lax.ppermute(
        jnp.concatenate([flat, jnp.concatenate([to_gm, pad8], axis=0)], axis=1), "group", down
    )
    from_gm = lax.ppermute(
        jnp.concatenate([flat, jnp.concatenate([to_gp, pad8], axis=0)], axis=1), "group", up
    )
    (inv,) = call(
        invert_kernel,
        (sds((2, ND, ND)),),
        (),
        factor[0],
        scratch=[pltpu.VMEM((2 * NCH, LN, LN), F32), pltpu.VMEM((2 * NCH, LN, LN), F32)],
        flops=20_000_000_000,
        name="invert",
    )
    wide = 12 * DEV
    table = jnp.concatenate(
        [flat, from_right[:, :wide], from_left[:, :wide], from_gm[:, :wide], from_gp[:, :wide]], axis=0
    )
    near = jnp.stack(
        [from_left[:, wide:], from_right[:, wide:], from_gm[0:8, wide:], from_gp[0:8, wide:]]
    )
    (ar,) = call(spread_kernel, (sds((2, 40, ND)),), (), rface, near, own, tt, name="spread")
    st_s, o_s, hs_s, pay_s = sds((12, ND)), sds((2, 256)), sds((24, DEV)), sds((DEV, 2 * LN))
    st, o, pay = call(
        begin_kernel, (st_s, o_s, pay_s), (0,), pos, recv0, loads, inv, tt, ar, table, aux, name="begin"
    )
    st, o, pay = call(
        first_kernel, (st_s, o_s, pay_s), (0,), pos, exchange(pay), st, o, inv, tt, ar, table, aux,
        name="first",
    )
    hs = jnp.zeros((24, DEV), F32)
    for it in range(ITERS - 1):
        st, o, hs, pay = call(
            make_step(it), (st_s, o_s, hs_s, pay_s), (0,),
            pos, exchange(pay), st, o, hs, inv, tt, ar, table, aux, name=f"step{it}",
        )
    lam, proj = call(
        last_kernel, (sds((2, ND)), sds((2, ND))), (0,),
        pos, exchange(pay), st, o, hs, tt, ar, table, aux, qt, name="last",
    )
    return lam[None], proj[None]


def solution(mesh):
    return jax.shard_map(
        shards,
        mesh=mesh,
        in_specs=(
            P("group", "member", None, None),
            P("group", "member", None),
            P("group", "member", None),
            P("group", "member", None),
            P("group", "member"),
            P("group", "member", None, None),
            P("group", "member", None),
            P("group", "member", None, None),
            P(("group", "member"), None),
        ),
        out_specs=(P("group", "member", None), P("group", "member", None)),
        check_vma=False,
    )
```

time: 2200 us -> 168 us (0.08)
  other arithmetic: 636 us -> 0.22 us
  blocking collectives: 675 us -> 93.7 us
  starting transfers between devices: 443 us -> 26 us
  local copies, waits for them, and re-layouts: 255 us -> 20.6 us
  matrix products: 109 us -> 0 us
  waiting for transfers between devices: 47.8 us -> 0.03 us
  Pallas kernels: 0 us -> 26 us
    another operation x63 -> x2, other arithmetic: 620 us -> 0.08 us  [the longest x1 0.08 us: shards(): jnp.stack([jnp.where(m > 0, me - 1, me), jnp.where(m < 15, me + 1, me), j...]
    ppermute x39 -> x4, starting transfers between devices: 443 us -> 10.3 us  [the longest x1 4.05 us: shards(): lax.ppermute(jnp.concatenate([rows[0], rface[0][:, :LN]], axis=1), 'membe...]
    psum x5 -> x0, blocking collectives: 392 us -> none  [global_sum(): return lax.psum(partial_value, ('group', 'member'))]
    all_gather x5 -> x0, blocking collectives: 283 us -> none  [gather_coarse(): lax.all_gather(local_coarse.reshape(1, -1), ('group', 'member'), axis=0,...]
    another operation x185 -> x5, local copies, waits for them, and re-layouts: 149 us -> 0.78 us  [the longest x1 0.77 us: shards(): slots = face_slot[0].reshape(2, 256)]
    all_to_all x0 -> x4, blocking collectives: none -> 93.7 us  [exchange(): return lax.all_to_all(pay, axes, 0, 0, tiled=True)]
    gather x6 -> x0, local copies, waits for them, and re-layouts: 84.6 us -> none  [the longest x3 71.1 us: shards(): jnp.take_along_axis(mode_table, jnp.broadcast_to(dof_map[0][:, None, :],...]
    dot_general x45 -> x0, matrix products: 64.5 us -> none  [the longest x8 26.2 us: product_block(): lax.dot_general(solved, solved_piece, (((0,), (0,)), ((), ())), precision...]
  transfers between devices with their start and end apart: 39 -> 5, of which waited for: 17 -> 0; matrix products, arithmetic and copies ran while one was open for 40% -> 4% of each run, Pallas kernels for 0% -> 8%
where the time goes in v1:
time: 168 us; the launch traced here: 167 us
  blocking collectives  93.7 us (56%)
  Pallas kernels  26 us (15%)
  starting transfers between devices  26 us (15%)
  local copies, waits for them, and re-layouts  20.6 us (12%)
    all_to_all x4, blocking collectives, exchange(): return lax.all_to_all(pay, axes, 0, 0, tiled=True)  93.7 us
    pallas_call x8, Pallas kernels, call(): pl.pallas_call(kernel, out_shape=outs, in_specs=specs, out_specs=tuple((V...  26 us
    all_to_all x1, starting transfers between devices, exchange(): return lax.all_to_all(pay, axes, 0, 0, tiled=True)  15.6 us
    unnamed x33, local copies, waits for them, and re-layouts  11.8 us
    ppermute x1, starting transfers between devices, shards(): lax.ppermute(jnp.concatenate([rows[0], rface[0][:, :LN]], axis=1), 'membe...  4.05 us
    reshape x2, local copies, waits for them, and re-layouts, shards(): coarse_inverse.reshape(12, DEV, 12).transpose(0, 2, 1)  3.89 us
  transfers between devices with their start and end apart: 5, of which 0 were waited for; matrix products, arithmetic and copies ran while one was open for 4% of the time, Pallas kernels for 8%

profile of v1, /device:TPU:1, one launch (start us, length us, event | category | flops | bytes accessed | tf_op | source)
XLA Modules:
  0.0 167.5 jit_solution(11722493915458949615)
XLA Ops:
  0.6 0.8 reshape_squeeze.3.slot_ref
  1.5 0.7 lt.42
  2.3 0.7 copy.35
  3.0 0.7 copy-done.4
  3.7 0.7 copy-done.6
  4.4 0.7 copy-done.7
  5.1 0.7 copy-done.8
  5.8 3.4 %tables.1 = (bf16[2,768,256]{2,1,0:T(8,128)(2,1)S(1)}, bf16[2,768,768]{2,1,0:T(8,128)(2,1)S(1)}, f32[2,8,256]{2,1,0:T(8,128)S(1)}, f32[2,8,768]{2,1,0:T(8,128)S(...) custom-call(f32[2,768]{1,0:T(2,128)S(1)} %bitcast.68, s32[2,768]{1,0:T(2,128)S(1)} %bitcast.70, s32[2,768]{1,0:T(2,128)S(1)} %bitcast.71, ...), custom_call_target="tpu_custom_call" | custom-call | tf_op jit(solution)/shard_map/tables/pallas_call | solution.py:432
  9.1 1.4 copy-done.2
  10.6 15.6 %all-to-all-start = ((f32[256,1,128]{2,1,0:T(1,128)}), f32[256,1,128]{2,1,0:T(1,128)S(1)}, u32[]{:S(2)}, u32[]{:S(2)}) async-start(f32[256,1,128]{2,1,0:T(1,128)} %bitcast.11), calls=%async_computation | async-start | bytes 262144 | tf_op jit(solution)/shard_map/all_to_all | solution.py:475
  26.3 3.8 %reshape.27 = f32[12,256,12]{2,1,0:T(8,128)} reshape(f32[12,3072]{1,0:T(8,128)} %param.17) | data formatting | bytes 294912 | tf_op jit(solution)/shard_map/reshape | solution.py:478
  30.1 1.9 %copy.17 = f32[12,12,256]{2,1,0:T(8,128)S(1)} copy(f32[12,12,256]{1,2,0:T(8,128)} %bitcast.74) | data formatting | bytes 294912 | tf_op jit(solution)/shard_map/transpose | solution.py:478
  32.3 4.1 %collective-permute-start.1 = (f32[8,3200]{1,0:T(8,128)S(1)}, f32[8,3200]{1,0:T(8,128)S(1)}, u32[]{:S(2)}, u32[]{:S(2)}) collective-permute-start(f32[8,3200]{1,0:T(8,128)S(1)} %pad_maximum_fusion.1), channel_id=1, source_target_pairs={{1,0},{2,1},{3,2},{4,3},{5,4},{6,5},{7,6},{8,7},{9,8},{10,9},{11,1... | collective-permute-start | bytes 307208 | tf_op jit(solution)/shard_map/ppermute | solution.py:486
  36.4 1.9 %collective-permute-start = (f32[8,3200]{1,0:T(8,128)S(1)}, f32[8,3200]{1,0:T(8,128)S(1)}, u32[]{:S(2)}, u32[]{:S(2)}) collective-permute-start(f32[8,3200]{1,0:T(8,128)S(1)} %pad_maximum_fusion), channel_id=1, source_target_pairs={{0,1},{1,2},{2,3},{3,4},{4,5},{5,6},{6,7},{7,8},{8,9},{9,10},{10,1... | collective-permute-start | bytes 307208 | tf_op jit(solution)/shard_map/ppermute | solution.py:487
  38.4 2.9 %collective-permute-start.2 = (f32[16,3200]{1,0:T(8,128)S(1)}, f32[16,3200]{1,0:T(8,128)S(1)}, u32[]{:S(2)}, u32[]{:S(2)}) collective-permute-start(f32[16,3200]{1,0:T(8,128)S(1)} %get-tuple-element.48), channel_id=1, source_target_pairs={{0,16},{16,32},{32,48},{48,64},{64,80},{80,96},{96,112},{112,128},... | collective-permute-start | bytes 614408 | tf_op jit(solution)/shard_map/ppermute | solution.py:493
  41.2 1.5 collective-permute-start.3
  42.8 2.3 %copy-done.9 = f32[1,2,768,768]{3,2,1,0:T(8,128)S(1)} copy-done((f32[1,2,768,768]{3,2,1,0:T(8,128)S(1)}, f32[1,2,768,768]{3,2,1,0:T(8,128)}, u32[]{:S(2)}) %copy-start.9) | copy-done | bytes 4718616
  45.1 13.7 %invert.1.inv_ref = f32[2,768,768]{2,1,0:T(8,128)S(1)} custom-call(f32[2,768,768]{2,1,0:T(8,128)S(1)} %bitcast.73), custom_call_target="tpu_custom_call" | custom-call | flops 20000000000 | bytes 1048576 | tf_op jit(solution)/shard_map/invert/pallas_call | solution.py:432
  58.8 2.1 %copy-done = f32[2,768,768]{2,1,0:T(8,128)} copy-done((f32[2,768,768]{2,1,0:T(8,128)}, f32[2,768,768]{2,1,0:T(8,128)S(1)}, u32[]{:S(2)}) %copy-start) | copy-done | bytes 4718616
  61.2 0.3 spread.1.ar_ref
  61.5 2.3 %copy-done.1 = f32[2,768,768]{2,1,0:T(8,128)S(1)} copy-done((f32[2,768,768]{2,1,0:T(8,128)S(1)}, f32[2,768,768]{2,1,0:T(8,128)}, u32[]{:S(2)}) %copy-start.1) | copy-done | bytes 4718616
  63.9 1.6 begin.1
  65.5 0.3 copy.18
  65.7 29.8 %all_to_all.55 = f32[256,1,256]{2,1,0:T(1,128)S(1)} all-to-all(f32[256,1,256]{2,1,0:T(1,128)S(1)} %copy.18), channel_id=1, replica_groups=mesh['group'=16,'member'=16] {'group','member'}, dimensions={0} | all-to-all | bytes 524288 | tf_op jit(solution)/shard_map/all_to_all | solution.py:475
  95.6 1.6 first.1
  97.6 21.2 %all_to_all.56 = f32[256,1,256]{2,1,0:T(1,128)S(1)} all-to-all(f32[256,1,256]{2,1,0:T(1,128)S(1)} %copy.19), channel_id=1, replica_groups=mesh['group'=16,'member'=16] {'group','member'}, dimensions={0} | all-to-all | bytes 524288 | tf_op jit(solution)/shard_map/all_to_all | solution.py:475
  118.8 1.7 step0.1
  120.8 21.4 %all_to_all.57 = f32[256,1,256]{2,1,0:T(1,128)S(1)} all-to-all(f32[256,1,256]{2,1,0:T(1,128)S(1)} %copy.20), channel_id=1, replica_groups=mesh['group'=16,'member'=16] {'group','member'}, dimensions={0} | all-to-all | bytes 524288 | tf_op jit(solution)/shard_map/all_to_all | solution.py:475
  142.2 1.7 %step1.1 = (f32[12,768]{1,0:T(8,128)S(1)}, f32[2,256]{1,0:T(2,128)S(1)}, f32[24,256]{1,0:T(8,128)S(1)}, f32[256,256]{1,0:T(8,128)S(1)}) custom-call(s32[4]{0:T(128)S(1)} %pad_add_fusion.pos_ref, f32[256,256]{1,0:T(8,128)S(1)} %bitcast.60, f32[12,768]{1,0:T(8,128)S(1)} %get-tuple-element.36.st_ref, f32[2,256]{1,0:T(2,128)S(1)} %get-tuple-element.37.o_ref, ...), custom_call_target="tpu_custom_call" | custom-call | tf_op jit(solution)/shard_map/step1/pallas_call | solution.py:432
  143.9 0.3 copy.21
  144.2 21.2 %all_to_all.58 = f32[256,1,256]{2,1,0:T(1,128)S(1)} all-to-all(f32[256,1,256]{2,1,0:T(1,128)S(1)} %copy.21), channel_id=1, replica_groups=mesh['group'=16,'member'=16] {'group','member'}, dimensions={0} | all-to-all | bytes 524288 | tf_op jit(solution)/shard_map/all_to_all | solution.py:475
  165.4 2.1 %last.1 = (f32[2,768]{1,0:T(2,128)}, f32[2,768]{1,0:T(2,128)}) custom-call(s32[4]{0:T(128)S(1)} %pad_add_fusion.pos_ref, f32[256,256]{1,0:T(8,128)S(1)} %bitcast.58, f32[12,768]{1,0:T(8,128)S(1)} %get-tuple-element.40.st_ref, f32[2,256]{1,0:T(2,128)S(1)} %get-tuple-element.41.o_ref, f32[24,256]{1,0:T(8,128)S(1)} %get-tuple-element.42.hs_ref, ...), custom_call_target="tpu_custom_call" | custom-call | tf_op jit(solution)/shard_map/last/pallas_call | solution.py:432
  (55 shorter events, 1.4 us)
Async XLA Ops:
  3.0 0.7 copy-start.4
  3.7 0.7 copy-start.6
  4.4 0.7 copy-start.7
  5.1 0.7 copy-start.8
  9.1 1.5 copy-start.2
  10.6 50.9 %all-to-all-start = ((f32[256,1,128]{2,1,0:T(1,128)}), f32[256,1,128]{2,1,0:T(1,128)S(1)}, u32[]{:S(2)}, u32[]{:S(2)}) async-start(f32[256,1,128]{2,1,0:T(1,128)} %bitcast.11), calls=%async_computation | async-start | bytes 262144 | tf_op jit(solution)/shard_map/all_to_all | solution.py:475
  32.3 28.7 %collective-permute-start.1 = (f32[8,3200]{1,0:T(8,128)S(1)}, f32[8,3200]{1,0:T(8,128)S(1)}, u32[]{:S(2)}, u32[]{:S(2)}) collective-permute-start(f32[8,3200]{1,0:T(8,128)S(1)} %pad_maximum_fusion.1), channel_id=1, source_target_pairs={{1,0},{2,1},{3,2},{4,3},{5,4},{6,5},{7,6},{8,7},{9,8},{10,9},{11,1... | collective-permute-start | bytes 307208 | tf_op jit(solution)/shard_map/ppermute | solution.py:486
  36.4 24.6 %collective-permute-start = (f32[8,3200]{1,0:T(8,128)S(1)}, f32[8,3200]{1,0:T(8,128)S(1)}, u32[]{:S(2)}, u32[]{:S(2)}) collective-permute-start(f32[8,3200]{1,0:T(8,128)S(1)} %pad_maximum_fusion), channel_id=1, source_target_pairs={{0,1},{1,2},{2,3},{3,4},{4,5},{5,6},{6,7},{7,8},{8,9},{9,10},{10,1... | collective-permute-start | bytes 307208 | tf_op jit(solution)/shard_map/ppermute | solution.py:487
  38.4 22.7 %collective-permute-start.2 = (f32[16,3200]{1,0:T(8,128)S(1)}, f32[16,3200]{1,0:T(8,128)S(1)}, u32[]{:S(2)}, u32[]{:S(2)}) collective-permute-start(f32[16,3200]{1,0:T(8,128)S(1)} %get-tuple-element.48), channel_id=1, source_target_pairs={{0,16},{16,32},{32,48},{48,64},{64,80},{80,96},{96,112},{112,128},... | collective-permute-start | bytes 614408 | tf_op jit(solution)/shard_map/ppermute | solution.py:493
  41.2 19.9 %collective-permute-start.3 = (f32[16,3200]{1,0:T(8,128)S(1)}, f32[16,3200]{1,0:T(8,128)S(1)}, u32[]{:S(2)}, u32[]{:S(2)}) collective-permute-start(f32[16,3200]{1,0:T(8,128)S(1)} %get-tuple-element.49), channel_id=1, source_target_pairs={{16,0},{32,16},{48,32},{64,48},{80,64},{96,80},{112,96},{128,112},... | collective-permute-start | bytes 614408 | tf_op jit(solution)/shard_map/ppermute | solution.py:490
  42.8 2.3 %copy-start.9 = (f32[1,2,768,768]{3,2,1,0:T(8,128)S(1)}, f32[1,2,768,768]{3,2,1,0:T(8,128)}, u32[]{:S(2)}) copy-start(f32[1,2,768,768]{3,2,1,0:T(8,128)} %param.9) | copy-start | bytes 14155780
  45.1 16.4 %copy-start.5 = (f32[1,2,768]{2,1,0:T(2,128)S(1)}, f32[1,2,768]{2,1,0:T(2,128)}, u32[]{:S(2)}) copy-start(f32[1,2,768]{2,1,0:T(2,128)} %param.10) | copy-start | bytes 18436
  58.8 2.2 %copy-start = (f32[2,768,768]{2,1,0:T(8,128)}, f32[2,768,768]{2,1,0:T(8,128)S(1)}, u32[]{:S(2)}) copy-start(f32[2,768,768]{2,1,0:T(8,128)S(1)} %invert.1.inv_ref) | copy-start | bytes 14155780
  61.2 34.5 %slice-start = ((s8[4718592]{0:T(1024)(128)(4,1)}), s8[524288]{0:T(1024)(128)(4,1)S(1)}, s32[]{:S(2)}) async-start(s8[4718592]{0:T(1024)(128)(4,1)} %bitcast.56), calls=%async_computation.5 | async-start | bytes 1048576
  61.5 2.3 %copy-start.1 = (f32[2,768,768]{2,1,0:T(8,128)S(1)}, f32[2,768,768]{2,1,0:T(8,128)}, u32[]{:S(2)}) copy-start(f32[2,768,768]{2,1,0:T(8,128)} %copy-done) | copy-start | bytes 14155780
  63.9 31.8 %slice-start.1 = ((s8[4718592]{0:T(1024)(128)(4,1)}), s8[4194304]{0:T(1024)(128)(4,1)S(1)}, s32[]{:S(2)}) async-start(s8[4718592]{0:T(1024)(128)(4,1)} %bitcast.56), calls=%async_computation.6 | async-start | bytes 8388608
  120.8 44.7 %copy-start.3 = (bf16[2,768,768]{2,1,0:T(8,128)(2,1)S(1)}, bf16[2,768,768]{2,1,0:T(8,128)(2,1)}, u32[]{:S(2)}) copy-start(bf16[2,768,768]{2,1,0:T(8,128)(2,1)} %copy-done.2) | copy-start | bytes 7077892

commit v2 on v1

v2 whole, which is shorter than its diff:
```python
import jax
import jax.numpy as jnp
from jax import lax
from jax.experimental import pallas as pl
from jax.experimental.pallas import tpu as pltpu
from jax.sharding import PartitionSpec as P

ITERS = 3
ND = 768
LN = 128
NCH = ND // LN
DEV = 256
BASE = 16
F32 = jnp.float32
BF = jnp.bfloat16
NT = (((1,), (1,)), ((), ()))


def iota(shape, dim):
    return lax.broadcasted_iota(jnp.int32, shape, dim)


def coarse_kernel(load_hbm, node_hbm, modes_ref, pay_ref, load_ref, node_ref, sems):
    copies = [
        pltpu.make_async_copy(node_hbm, node_ref, sems.at[0]),
        pltpu.make_async_copy(load_hbm, load_ref, sems.at[1]),
    ]
    for c in copies:
        c.start()
    lane8 = iota((8, LN), 1)
    sub8 = iota((8, LN), 0)
    part = iota((8, ND), 0)
    row = jnp.zeros((1, LN), F32)
    dim = iota((1, ND), 1).astype(F32)
    node = jnp.floor((dim + 0.5) * (1.0 / 3.0))
    comp = dim - 3.0 * node
    first = (comp == 0.0).astype(F32)
    second = (comp == 1.0).astype(F32)
    third = (comp == 2.0).astype(F32)
    delta = iota((256, ND), 1) - 3 * iota((256, ND), 0)
    rep = jnp.where((delta >= 0) & (delta < 3), 1.0, 0.0).astype(BF)
    for c in copies:
        c.wait()
    for s in range(2):
        position = (node_ref[0, :, s, :].astype(F32) - 8.0) * 0.125
        spread = jnp.dot(position.astype(BF), rep, preferred_element_type=F32)
        cx = spread[0:1, :]
        cy = spread[1:2, :]
        cz = spread[2:3, :]
        rows = (
            first, second, third,
            third * cy - second * cz,
            first * cz - third * cx,
            second * cx - first * cy,
        )
        modes = jnp.zeros((8, ND), F32)
        for a in range(6):
            modes = jnp.where(part == a, rows[a], modes)
        modes_ref[s] = modes
        e = jnp.sum(modes * load_ref[0, s : s + 1, :], axis=1, keepdims=True)
        row = row + jnp.sum(jnp.where(lane8 == sub8 + 8 * s, e, 0.0), axis=0, keepdims=True)
    pay_ref[...] = jnp.broadcast_to(row, (DEV, LN))


def tables_kernel(
    modes_ref, load_hbm, map_hbm, sign_hbm, live_hbm, slot_hbm, count_hbm, coarse_hbm,
    tt_ref, qt_hbm, own_hbm, aux_ref, left_ref, right_ref, gm_ref, gp_ref,
    load_ref, map_ref, sign_ref, live_ref, slot_ref, count_ref, coarse_ref, own_ref, qt_ref, sems,
):
    copies = [
        pltpu.make_async_copy(src, dst, sems.at[i])
        for i, (src, dst) in enumerate(
            (
                (load_hbm, load_ref), (map_hbm, map_ref), (sign_hbm, sign_ref),
                (live_hbm, live_ref), (slot_hbm, slot_ref), (count_hbm, count_ref),
                (coarse_hbm, coarse_ref),
            )
        )
    ]
    for c in copies:
        c.start()
    part = iota((8, ND), 0)
    for c in copies[:-1]:
        c.wait()
    faces = []
    late = []
    for s in range(2):
        live = iota((1, ND), 1) < live_ref[0:1, s : s + 1]
        live_f = jnp.where(live, 1.0, 0.0)
        sgn = jnp.where(live, sign_ref[0, s : s + 1, :].astype(F32), 0.0)
        dof = map_ref[0, s : s + 1, :]
        dof_f = dof.astype(F32)
        high = jnp.floor(dof_f * (1.0 / 32.0))
        low = dof_f - 32.0 * high
        lhs = jnp.where(part == 0, high, jnp.where(part == 1, low, jnp.where(part == 2, sgn, 0.0)))
        pos64 = iota((1, 64), 1)
        slots = jnp.concatenate(
            [
                jnp.where(pos64 < count_ref[0, s : s + 1, f : f + 1], slot_ref[0, s, f : f + 1, :], -1)
                for f in range(4)
            ],
            axis=1,
        )
        hit = jnp.where(iota((ND, 256), 0) == slots, 1.0, 0.0).astype(BF)
        got = jnp.dot(lhs.astype(BF), hit, preferred_element_type=F32)
        dk = (32.0 * got[0:1, :] + got[1:2, :]).astype(jnp.int32)
        sk = got[2:3, :]
        tt = jnp.where(iota((ND, 256), 0) == dk, sk, 0.0)
        tt_b = tt.astype(BF)
        tt_ref[s] = tt_b
        qt = jnp.where(iota((ND, ND), 0) == dof, 1.0, 0.0).astype(BF)
        qt_ref[s] = qt
        qt_copy = pltpu.make_async_copy(qt_ref.at[s], qt_hbm.at[s], sems.at[8 + s])
        qt_copy.start()
        late.append(qt_copy)
        mask = lax.dot_general(
            jnp.broadcast_to(live_f, (8, ND)).astype(BF), qt, NT, preferred_element_type=F32
        )[0:1, :]
        count = lax.dot_general(
            jnp.ones((8, 256), BF), jnp.abs(tt).astype(BF), NT, preferred_element_type=F32
        )[0:1, :]
        aux_ref[s : s + 1, :] = mask
        aux_ref[2 + s : 3 + s, :] = mask * (1.0 - 0.5 * count)
        aux_ref[4 + s : 5 + s, :] = sgn
        aux_ref[6 + s : 7 + s, :] = load_ref[0, s : s + 1, :]
        modes = modes_ref[s]
        own_ref[s, 0:8, :] = modes * mask
        face = jnp.dot(modes.astype(BF), tt_b, preferred_element_type=F32)
        own_ref[s, 8:16, :] = jnp.concatenate([face, jnp.zeros((8, ND - 256), F32)], axis=1)
        faces.append(face)
    wide = 12 * DEV
    to_left, to_right, to_gm, to_gp = pack_faces(faces[0], faces[1])
    left_ref[:, wide:] = to_left
    right_ref[:, wide:] = to_right
    zero = jnp.zeros((8, LN), F32)
    gm_ref[0:8, wide:] = to_gm
    gp_ref[0:8, wide:] = to_gp
    gm_ref[8:16, wide:] = zero
    gp_ref[8:16, wide:] = zero
    own_copy = pltpu.make_async_copy(own_ref, own_hbm, sems.at[7])
    own_copy.start()
    late.append(own_copy)
    copies[-1].wait()
    perm = jnp.where(
        (iota((384, 384), 0) - 12 * (iota((384, 384), 1) % 32)) == iota((384, 384), 1) // 32, 1.0, 0.0
    ).astype(BF)
    keep = iota((8, 384), 0) < 6
    res = []
    for q in range(8):
        c = coarse_ref[:, 384 * q : 384 * (q + 1)]
        c16 = jnp.concatenate([c, jnp.zeros((4, 384), F32)], axis=0)
        up = jnp.where(keep, c16[0:8], 0.0)
        dn = jnp.where(keep, pltpu.roll(c16, 10, 0)[0:8], 0.0)
        both = jnp.concatenate([up, dn], axis=0)
        h = both.astype(BF)
        rest = both - h.astype(F32)
        m = rest.astype(BF)
        l = (rest - m.astype(F32)).astype(BF)
        got = jnp.dot(jnp.concatenate([h, m, l], axis=0), perm, preferred_element_type=F32)
        res.append(got[0:16] + got[16:32] + got[32:48])
    quarter = iota((16, LN), 1) // 32
    for v in range(12):
        for half in range(2):
            acc = None
            for i in range(4):
                src = res[4 * half + i][:, LN * (v // 4) : LN * (v // 4 + 1)]
                shift = (32 * (i - v % 4)) % LN
                src = pltpu.roll(src, shift, 1) if shift else src
                acc = src if acc is None else jnp.where(quarter == i, src, acc)
            at = v * DEV + half * LN
            left_ref[:, at : at + LN] = acc[0:8]
            right_ref[:, at : at + LN] = acc[8:16]
            gm_ref[:, at : at + LN] = acc
            gp_ref[:, at : at + LN] = acc
    for c in late:
        c.wait()


def half_masks(rows):
    return iota((rows, LN), 1) < 64


def pack_faces(o0, o1):
    lo = half_masks(o0.shape[0])
    o0l, o0h, o1l, o1h = o0[:, :LN], o0[:, LN:], o1[:, :LN], o1[:, LN:]
    to_gm = jnp.where(lo, o0h, pltpu.roll(o1h, 64, 1))
    to_gp = jnp.where(lo, pltpu.roll(o0h, 64, 1), o1h)
    return o0l, o1l, to_gm, to_gp


def spread(near, own_ref, tt_ref, ar_ref):
    lo = half_masks(8)
    zero = jnp.zeros((8, LN), F32)
    left, right, gm, gp = near
    r0l, r1l = own_ref[0, 8:16, 0:LN], own_ref[1, 8:16, 0:LN]

    def both(a, b):
        return jnp.concatenate([a, b], axis=1)

    w0 = [
        both(zero, zero),
        both(pltpu.roll(jnp.where(lo, r1l, 0.0), 64, 1), zero),
        both(pltpu.roll(jnp.where(lo, 0.0, left), 64, 1), zero),
        both(zero, jnp.where(lo, gm, 0.0)),
        both(zero, jnp.where(lo, 0.0, pltpu.roll(gp, 64, 1))),
    ]
    w1 = [
        both(pltpu.roll(jnp.where(lo, 0.0, r0l), 64, 1), zero),
        both(zero, zero),
        both(pltpu.roll(jnp.where(lo, right, 0.0), 64, 1), zero),
        both(zero, jnp.where(lo, pltpu.roll(gm, 64, 1), 0.0)),
        both(zero, jnp.where(lo, 0.0, gp)),
    ]
    for s, w in ((0, w0), (1, w1)):
        table = jnp.concatenate(w, axis=0).astype(BF)
        ar_ref[s] = lax.dot_general(table, tt_ref[s], NT, preferred_element_type=F32)
        at = 8 * s
        ar_ref[s, at : at + 8, :] = own_ref[s, 0:8, :]


def two(a):
    h = a.astype(BF)
    return h, (a - h.astype(F32)).astype(BF)


def mm3(a, b):
    ah, al = two(a)
    bh, bl = two(b)

    def d(x, y):
        return jnp.dot(x, y, preferred_element_type=F32)

    return d(ah, bh) + (d(ah, bl) + d(al, bh))


def invert_kernel(l_hbm,out_hbm,out_ref,l_ref,d_ref,x_ref,sem_d,sem_l,sem_o):
    copies_d=[pltpu.make_async_copy(l_hbm.at[0,s,pl.ds(b*LN,LN),pl.ds(b*LN,LN)],d_ref.at[s*NCH+b],sem_d.at[s*NCH+b]) for s in range(2) for b in range(NCH)]
    for c in copies_d: c.start()
    copies_l=[pltpu.make_async_copy(l_hbm.at[0,s,pl.ds(b*LN,LN),pl.ds(0,b*LN)],l_ref.at[s,pl.ds(b*LN,LN),pl.ds(0,b*LN)],sem_l.at[s*NCH+b]) for s in range(2) for b in range(1,NCH)]
    for c in copies_l: c.start()
    ri=iota((LN,LN),0); ci=iota((LN,LN),1); eye=ri==ci; below=ri>ci
    lane=iota((BASE,LN),1); row=iota((BASE,LN),0)
    nb=2*NCH; ng=LN//BASE
    group=(lane//BASE)*BASE
    for c in copies_d: c.wait()
    packs=[]
    for k in range(nb):
        lb=d_ref[k]
        diag=jnp.sum(jnp.where(eye,lb,0.0),axis=1,keepdims=True)
        n=jnp.where(below,lb*(1.0/diag),0.0)
        rowdiag=jnp.sum(jnp.where(eye,lb,0.0),axis=0,keepdims=True)
        d_ref[k]=n
        x_ref[k,0:1,:]=1.0/rowdiag
        p=None
        for g in range(ng):
            t=jnp.where(lane//BASE==g,n[g*BASE:(g+1)*BASE,:],0.0)
            p=t if p is None else p+t
        packs.append(p)
    xs=[jnp.where(row==lane%BASE,1.0,0.0) for _ in range(nb)]
    for j in range(BASE-1):
        lo=(j+1)//8*8
        for k in range(nb):
            idx=group[lo:,:]+j
            f=jnp.take_along_axis(packs[k][lo:,:],idx,axis=1)
            new=xs[k][lo:,:]-f*xs[k][j:j+1,:]
            xs[k]=new if lo==0 else jnp.concatenate([xs[k][:lo,:],new],axis=0)
    invd=[x_ref[k,0:1,:] for k in range(nb)]
    for k in range(nb):
        for g in range(ng):
            x_ref[k,g*BASE:(g+1)*BASE,:]=jnp.where(lane//BASE==g,xs[k],0.0)
    z=jnp.zeros((LN,LN),F32)

    def bd(a,b):
        return jnp.concatenate([jnp.concatenate([a,z],axis=1),jnp.concatenate([z,b],axis=1)],axis=0)

    size=BASE
    while size<LN:
        pick=((ri//(2*size))==(ci//(2*size)))&((ri//size)!=(ci//size))
        ts=[]
        for q in range(nb//2):
            e=jnp.concatenate([jnp.where(pick,d_ref[2*q],0.0),jnp.where(pick,d_ref[2*q+1],0.0)],axis=1)
            ts.append(mm3(e,bd(x_ref[2*q],x_ref[2*q+1])))
        for q in range(nb//2):
            xc=jnp.concatenate([x_ref[2*q],x_ref[2*q+1]],axis=1)
            xn=xc-mm3(xc,bd(ts[q][:,:LN],ts[q][:,LN:]))
            x_ref[2*q]=xn[:,:LN]; x_ref[2*q+1]=xn[:,LN:]
        size*=2
    for k in range(nb): x_ref[k]=x_ref[k]*invd[k]
    for c in copies_l: c.wait()

    def block(s,i,j,w=LN): return l_ref[s,i*w:(i+1)*w,j*w:(j+1)*w]

    sent=[]

    def send_block(s,i,j):
        src=out_ref.at[s,pl.ds(i*2*LN,2*LN),pl.ds(j*2*LN,2*LN)]
        dst=out_hbm.at[s,pl.ds(i*2*LN,2*LN),pl.ds(j*2*LN,2*LN)]
        c=pltpu.make_async_copy(src,dst,sem_o.at[len(sent)])
        c.start()
        sent.append(c)

    pairs=[(s,q) for s in range(2) for q in range(NCH//2)]
    mids={}
    for s,q in pairs:
        mids[s,q]=mm3(block(s,2*q+1,2*q),x_ref[s*NCH+2*q])
    for s,q in pairs:
        at=2*q*LN
        out_ref[s,at:at+LN,at:at+LN]=x_ref[s*NCH+2*q]
        out_ref[s,at:at+LN,at+LN:at+2*LN]=z
        out_ref[s,at+LN:at+2*LN,at:at+LN]=-mm3(x_ref[s*NCH+2*q+1],mids[s,q])
        out_ref[s,at+LN:at+2*LN,at+LN:at+2*LN]=x_ref[s*NCH+2*q+1]
        send_block(s,q,q)
    wd=2*LN

    def inv(s,i,j): return out_ref[s,i*wd:(i+1)*wd,j*wd:(j+1)*wd]

    a=[[mm3(block(s,i,i-1,wd),inv(s,i-1,i-1)) for i in (1,2)] for s in range(2)]
    b=[mm3(block(s,2,0,wd),inv(s,0,0)) for s in range(2)]
    for s in range(2):
        for i in (1,2):
            out_ref[s,i*wd:(i+1)*wd,(i-1)*wd:i*wd]=-mm3(inv(s,i,i),a[s][i-1])
            send_block(s,i,i-1)
    for s in range(2):
        m=b[s]+mm3(block(s,2,1,wd),inv(s,1,0))
        out_ref[s,2*wd:3*wd,0:wd]=-mm3(inv(s,2,2),m)
        send_block(s,2,0)
    for c in sent: c.wait()


def split3(rows, total):
    idx = iota((total, rows[0].shape[1]), 0)
    out = jnp.zeros((total, rows[0].shape[1]), F32)
    for r, z in enumerate(rows):
        h = z.astype(BF).astype(F32)
        rest = z - h
        m = rest.astype(BF).astype(F32)
        l = rest - m
        out = jnp.where(idx == 3 * r, h, out)
        out = jnp.where(idx == 3 * r + 1, m, out)
        out = jnp.where(idx == 3 * r + 2, l, out)
    return out.astype(BF)


def solve(inv_ref, s, z):
    ys = []
    for b in range(NCH):
        acc = None
        for c in range(b + 1):
            term = inv_ref[s, b * LN : (b + 1) * LN, c * LN : (c + 1) * LN] * z[:, c * LN : (c + 1) * LN]
            acc = term if acc is None else acc + term
        ys.append(jnp.sum(acc, axis=1, keepdims=True))
    us = []
    for c in range(NCH):
        acc = None
        for b in range(c, NCH):
            term = inv_ref[s, b * LN : (b + 1) * LN, c * LN : (c + 1) * LN] * ys[b]
            acc = term if acc is None else acc + term
        us.append(jnp.sum(acc, axis=0, keepdims=True))
    return jnp.concatenate(us, axis=1)


def received_coarse(recv_ref):
    xt = jnp.transpose(recv_ref[:, 0:LN])

    def grp(i):
        return xt[8 * i : 8 * i + 8, :]

    h0 = grp(0) + pltpu.roll(grp(2), 1, 1) + pltpu.roll(grp(4), DEV - 16, 1) + pltpu.roll(grp(6), 16, 1)
    h1 = grp(1) + pltpu.roll(grp(3), DEV - 1, 1) + pltpu.roll(grp(5), DEV - 16, 1) + pltpu.roll(grp(7), 16, 1)
    sums = jnp.sum(grp(8), axis=1, keepdims=True)
    return h0, h1, sums


def project_rows(h0, h1, m_ref, ar_ref):
    acc = jnp.zeros((64, DEV), F32)
    for v in range(12):
        h = h0 if v < 6 else h1
        a = v % 6
        acc = acc + m_ref[:, v * DEV : (v + 1) * DEV] * h[a : a + 1, :]
    al = jnp.sum(acc, axis=1, keepdims=True)

    def grp(i):
        return al[8 * i : 8 * i + 8, :]

    a0 = jnp.concatenate([grp(0), grp(1), grp(3), grp(4), grp(6)], axis=0)
    a1 = jnp.concatenate([grp(0), grp(1), grp(2), grp(5), grp(7)], axis=0)
    w0 = jnp.sum(ar_ref[0] * a0, axis=0, keepdims=True)
    w1 = jnp.sum(ar_ref[1] * a1, axis=0, keepdims=True)
    return w0, w1


def places():
    g = lax.axis_index("group")
    m = lax.axis_index("member")
    me = g * 16 + m
    return (
        jnp.where(m > 0, me - 1, me),
        jnp.where(m < 15, me + 1, me),
        jnp.where(g > 0, me - 16, me),
        jnp.where(g < 15, me + 16, me),
    )


def tile_of(row):
    base = pl.multiple_of((row // 8) * 8, 8)
    return base, row - base


def face_row(recv_ref, row):
    base, offset = tile_of(row)
    tile = recv_ref[pl.ds(base, 8), LN : 2 * LN]
    return jnp.sum(jnp.where(iota((8, LN), 0) == offset, tile, 0.0), axis=0, keepdims=True)


def assembled(recv_ref, y, o, tt_ref):
    lo = half_masks(1)
    left, right, gm, gp = (face_row(recv_ref, row) for row in places())
    o0l, o1l = o[0][:, :LN], o[1][:, :LN]
    in0 = jnp.concatenate(
        [pltpu.roll(jnp.where(lo, o1l, left), 64, 1), jnp.where(lo, gm, pltpu.roll(gp, 64, 1))], axis=1
    )
    in1 = jnp.concatenate(
        [pltpu.roll(jnp.where(lo, right, o0l), 64, 1), jnp.where(lo, pltpu.roll(gm, 64, 1), gp)], axis=1
    )
    out = []
    for s, inc in ((0, in0), (1, in1)):
        add = lax.dot_general(split3([inc], 8), tt_ref[s], NT, preferred_element_type=F32)
        out.append(y[s] + jnp.sum(add, axis=0, keepdims=True))
    return out


def send(pay_ref, y, tt_ref, ar_ref, dots):
    o = []
    cols = []
    for s in range(2):
        prod = jnp.dot(split3([y[s]], 8), tt_ref[s], preferred_element_type=F32)
        o.append(jnp.sum(prod, axis=0, keepdims=True))
        cols.append(jnp.sum(ar_ref[s] * y[s], axis=1, keepdims=True))
    c0, c1 = cols

    def grp(c, i):
        return c[8 * i : 8 * i + 8, :]

    cc = jnp.concatenate(
        [
            grp(c0, 0) + grp(c1, 0), grp(c0, 1) + grp(c1, 1), grp(c1, 2), grp(c0, 2),
            grp(c0, 3), grp(c1, 3), grp(c0, 4), grp(c1, 4),
        ],
        axis=0,
    )
    diag = iota((64, LN), 0) == iota((64, LN), 1)
    row = jnp.sum(jnp.where(diag, cc, 0.0), axis=0, keepdims=True)
    lane = iota((1, LN), 1)
    for i, value in enumerate(dots):
        row = jnp.where(lane == 64 + i, value, row)
    pay_ref[:, 0:LN] = jnp.broadcast_to(row, (DEV, LN))
    pay_ref[:, LN : 2 * LN] = jnp.zeros((DEV, LN), F32)
    to_left, to_right, to_gm, to_gp = pack_faces(o[0], o[1])
    for row, face in zip(places(), (to_left, to_right, to_gm, to_gp)):
        base, offset = tile_of(row)
        old = pay_ref[pl.ds(base, 8), LN : 2 * LN]
        pay_ref[pl.ds(base, 8), LN : 2 * LN] = jnp.where(iota((8, LN), 0) == offset, face, old)
    return o


def inner(a, b):
    return jnp.sum(a[0] * b[0] + a[1] * b[1], axis=1, keepdims=True)


def pair(ref, i):
    return [ref[i : i + 1, :], ref[i + 1 : i + 2, :]]


def put(ref, i, v):
    ref[i : i + 1, :] = v[0]
    ref[i + 1 : i + 2, :] = v[1]


LAM, PV, DV, IM, YD, YV = 0, 2, 4, 6, 8, 10


def begin_kernel(
    recv_ref, tt_ref, aux_ref, inv_hbm, own_hbm, mine_ref, near_ref,
    ar_ref, m_ref, st_ref, o_ref, pay_ref, inv_ref, own_ref, sems, sems_inv,
):
    wide = 12 * DEV
    own_copy = pltpu.make_async_copy(own_hbm, own_ref, sems.at[0])
    own_copy.start()
    parts = [
        pltpu.make_async_copy(
            inv_hbm.at[s, pl.ds(b * LN, LN), pl.ds(0, (b + 1) * LN)],
            inv_ref.at[s, pl.ds(b * LN, LN), pl.ds(0, (b + 1) * LN)],
            sems_inv.at[s * NCH + b],
        )
        for s in range(2)
        for b in range(NCH)
    ]
    for c in parts:
        c.start()
    h0, h1, _ = received_coarse(recv_ref)
    m_ref[0:16, :] = mine_ref[:, 0:wide]
    m_ref[16:64, :] = near_ref[:, 0:wide]
    own_copy.wait()
    near = [near_ref[at : at + 8, wide:] for at in (8, 0, 16, 32)]
    spread(near, own_ref, tt_ref, ar_ref)
    lam = project_rows(h0, h1, m_ref, ar_ref)
    mask = pair(aux_ref, 0)
    load = pair(aux_ref, 6)
    for c in parts:
        c.wait()
    y = [mask[s] * solve(inv_ref, s, load[s] - lam[s]) for s in range(2)]
    o = send(pay_ref, y, tt_ref, ar_ref, [])
    put(st_ref, LAM, lam)
    put(st_ref, YV, y)
    put(o_ref, 0, o)


def next_solve(pay_ref, inv_ref, tt_ref, ar_ref, aux_ref, p, d, yd):
    mask = pair(aux_ref, 0)
    weight = pair(aux_ref, 2)
    y = [mask[s] * solve(inv_ref, s, p[s]) for s in range(2)]
    wp = [weight[s] * p[s] for s in range(2)]
    dots = [inner(wp, p), inner(p, y)]
    if d is not None:
        dots += [inner(d, y), inner(p, yd)]
    o = send(pay_ref, y, tt_ref, ar_ref, dots)
    return y, o


def first_kernel(recv_ref, st_ref, o_ref, inv_ref, tt_ref, ar_ref, m_ref, aux_ref, st2_ref, o2_ref, pay_ref):
    h0, h1, _ = received_coarse(recv_ref)
    w = project_rows(h0, h1, m_ref, ar_ref)
    res = assembled(recv_ref, pair(st_ref, YV), pair(o_ref, 0), tt_ref)
    p = [res[s] - w[s] for s in range(2)]
    y, o = next_solve(pay_ref, inv_ref, tt_ref, ar_ref, aux_ref, p, None, None)
    put(st2_ref, LAM, pair(st_ref, LAM))
    put(st2_ref, PV, p)
    put(st2_ref, YV, y)
    put(o2_ref, 0, o)


def step_body(it, recv_ref, st_ref, o_ref, hs_ref, tt_ref, ar_ref, m_ref):
    h0, h1, sums = received_coarse(recv_ref)
    norm = sums[0:1, :]
    y = pair(st_ref, YV)
    p = pair(st_ref, PV)
    image = assembled(recv_ref, y, pair(o_ref, 0), tt_ref)
    if it == 0:
        d, yd, curve = p, y, sums[1:2, :]
    else:
        beta = norm / hs_ref[16:17, 0:1]
        curve = sums[1:2, :] + beta * (sums[2:3, :] + sums[3:4, :]) + beta * beta * hs_ref[17:18, 0:1]
        dold, iold, yold = pair(st_ref, DV), pair(st_ref, IM), pair(st_ref, YD)
        d = [p[s] + beta * dold[s] for s in range(2)]
        yd = [y[s] + beta * yold[s] for s in range(2)]
        image = [image[s] + beta * iold[s] for s in range(2)]
        h0 = h0 + beta * hs_ref[0:8, :]
        h1 = h1 + beta * hs_ref[8:16, :]
    step = norm / curve
    w = project_rows(h0, h1, m_ref, ar_ref)
    lam = pair(st_ref, LAM)
    lam = [lam[s] + step * d[s] for s in range(2)]
    pn = [p[s] - step * (image[s] - w[s]) for s in range(2)]
    return lam, pn, d, yd, image, h0, h1, norm, curve


def make_step(it):
    def step_kernel(
        recv_ref, st_ref, o_ref, hs_ref, inv_ref, tt_ref, ar_ref, m_ref, aux_ref,
        st2_ref, o2_ref, hs2_ref, pay_ref,
    ):
        lam, pn, d, yd, image, h0, h1, norm, curve = step_body(
            it, recv_ref, st_ref, o_ref, hs_ref, tt_ref, ar_ref, m_ref
        )
        y, o = next_solve(pay_ref, inv_ref, tt_ref, ar_ref, aux_ref, pn, d, yd)
        for at, v in ((LAM, lam), (PV, pn), (DV, d), (IM, image), (YD, yd), (YV, y)):
            put(st2_ref, at, v)
        put(o2_ref, 0, o)
        hs2_ref[0:8, :] = h0
        hs2_ref[8:16, :] = h1
        hs2_ref[16:17, :] = jnp.broadcast_to(norm, (1, DEV))
        hs2_ref[17:18, :] = jnp.broadcast_to(curve, (1, DEV))

    return step_kernel


def last_kernel(recv_ref, st_ref, o_ref, hs_ref, tt_ref, ar_ref, m_ref, aux_ref, qt_ref, lam_ref, p_ref):
    lam, pn = step_body(ITERS - 1, recv_ref, st_ref, o_ref, hs_ref, tt_ref, ar_ref, m_ref)[:2]
    for s in range(2):
        got = jnp.dot(split3([lam[s], pn[s]], 8), qt_ref[s], preferred_element_type=F32)
        sgn = aux_ref[4 + s : 5 + s, :]
        lam_ref[s : s + 1, :] = sgn * jnp.sum(got[0:3, :], axis=0, keepdims=True)
        p_ref[s : s + 1, :] = sgn * jnp.sum(got[3:6, :], axis=0, keepdims=True)


def sds(shape, dtype=F32):
    return jax.ShapeDtypeStruct(shape, dtype)


VM = pl.BlockSpec(memory_space=pltpu.VMEM)
HB = pl.BlockSpec(memory_space=pltpu.HBM)


def call(kernel, outs, specs, *args, scratch=(), flops=0, mib=16, hbm_outs=()):
    args = [
        pltpu.with_memory_space_constraint(x, pltpu.HBM) if specs.get(i) is HB else x for i, x in enumerate(args)
    ]
    return pl.pallas_call(
        kernel,
        out_shape=outs,
        in_specs=[specs.get(i, VM) for i in range(len(args))],
        out_specs=tuple(HB if i in hbm_outs else VM for i in range(len(outs))),
        scratch_shapes=list(scratch),
        compiler_params=pltpu.CompilerParams(vmem_limit_bytes=mib * 2**20),
        cost_estimate=pl.CostEstimate(flops=flops, transcendentals=0, bytes_accessed=2**20)
        if flops
        else None,
    )(*args)


def shards(factor, load, dof_map, dof_sign, live_count, face_slot, face_count, node_coord, coarse_inverse):
    axes = ("group", "member")
    packed = 12 * DEV + LN
    modes, pay0 = call(
        coarse_kernel,
        (sds((2, 8, ND)), sds((DEV, LN))),
        {0: HB, 1: HB},
        load, node_coord.transpose(0, 2, 1, 3),
        scratch=[
            pltpu.VMEM(load.shape, load.dtype), pltpu.VMEM((1, 3, 2, 256), node_coord.dtype),
            pltpu.SemaphoreType.DMA((2,)),
        ],
    )

    def exchange(pay):
        return lax.all_to_all(pay, axes, 0, 0, tiled=True)

    recv0 = exchange(pay0)
    raw = (load, dof_map, dof_sign, live_count, face_slot, face_count, coarse_inverse)
    tt, qt, own, aux, to_left, to_right, to_gm, to_gp = call(
        tables_kernel,
        (
            sds((2, ND, 256), BF), pltpu.HBM((2, ND, ND), BF), pltpu.HBM((2, 16, ND), F32), sds((8, ND)),
            sds((8, packed)), sds((8, packed)), sds((16, packed)), sds((16, packed)),
        ),
        {i: HB for i in range(1, 8)},
        modes, *raw,
        scratch=[pltpu.VMEM(r.shape, r.dtype) for r in raw]
        + [pltpu.VMEM((2, 16, ND), F32), pltpu.VMEM((2, ND, ND), BF), pltpu.SemaphoreType.DMA((10,))],
        hbm_outs=(1, 2),
    )

    up = [(i, i + 1) for i in range(15)]
    down = [(i + 1, i) for i in range(15)]
    from_right = lax.ppermute(to_left, "member", down)
    from_left = lax.ppermute(to_right, "member", up)
    from_gp = lax.ppermute(to_gm, "group", down)
    from_gm = lax.ppermute(to_gp, "group", up)
    (inv,) = call(
        invert_kernel,
        (pltpu.HBM((2, ND, ND), F32),),
        {0: HB},
        factor,
        scratch=[
            pltpu.VMEM((2, ND, ND), F32), pltpu.VMEM((2, ND, ND), F32), pltpu.VMEM((2 * NCH, LN, LN), F32),
            pltpu.VMEM((2 * NCH, LN, LN), F32), pltpu.SemaphoreType.DMA((2 * NCH,)),
            pltpu.SemaphoreType.DMA((2 * NCH,)), pltpu.SemaphoreType.DMA((2 * NCH,)),
        ],
        hbm_outs=(0,),
        flops=20_000_000_000,
        mib=24,
    )
    near = jnp.concatenate([from_right, from_left, from_gm, from_gp], axis=0)
    st_s, o_s, hs_s, pay_s = sds((12, ND)), sds((2, 256)), sds((24, DEV)), sds((DEV, 2 * LN))
    ar, table, st, o, pay = call(
        begin_kernel, (sds((2, 40, ND)), sds((64, 12 * DEV)), st_s, o_s, pay_s),
        {3: HB, 4: HB},
        recv0, tt, aux, inv, own, to_gm, near,
        scratch=[
            pltpu.VMEM((2, ND, ND), F32), pltpu.VMEM((2, 16, ND), F32),
            pltpu.SemaphoreType.DMA((1,)), pltpu.SemaphoreType.DMA((2 * NCH,)),
        ],
    )
    st, o, pay = call(first_kernel, (st_s, o_s, pay_s), {}, exchange(pay), st, o, inv, tt, ar, table, aux)
    hs = jnp.zeros((24, DEV), F32)
    for it in range(ITERS - 1):
        st, o, hs, pay = call(
            make_step(it), (st_s, o_s, hs_s, pay_s), {},
            exchange(pay), st, o, hs, inv, tt, ar, table, aux,
        )
    lam, proj = call(
        last_kernel, (sds((2, ND)), sds((2, ND))), {},
        exchange(pay), st, o, hs, tt, ar, table, aux, qt,
    )
    return lam[None], proj[None]


def solution(mesh):
    return jax.shard_map(
        shards,
        mesh=mesh,
        in_specs=(
            P("group", "member", None, None),
            P("group", "member", None),
            P("group", "member", None),
            P("group", "member", None),
            P("group", "member"),
            P("group", "member", None, None),
            P("group", "member", None),
            P("group", "member", None, None),
            P(("group", "member"), None),
        ),
        out_specs=(P("group", "member", None), P("group", "member", None)),
        check_vma=False,
    )
```

time: 168 us -> 146 us (0.87)
  local copies, waits for them, and re-layouts: 20.6 us -> 1.17 us
  blocking collectives: 93.7 us -> 89.1 us
  waiting for transfers between devices: 0.03 us -> 4.17 us
  Pallas kernels: 26 us -> 22 us
  starting transfers between devices: 26 us -> 27.9 us
    unnamed x33 -> x10, local copies, waits for them, and re-layouts: 11.8 us -> 0.08 us
    all_to_all x4, blocking collectives: 93.7 us -> 89.1 us  [exchange(): return lax.all_to_all(pay, axes, 0, 0, tiled=True)]
    all_to_all x1, waiting for transfers between devices: 0.02 us -> 4.16 us  [exchange(): return lax.all_to_all(pay, axes, 0, 0, tiled=True)]
    pallas_call x8, Pallas kernels: 26 us -> 22 us  [call(): pl.pallas_call(kernel, out_shape=outs, in_specs=[specs.get(i, VM) for i i...]
    reshape x3 -> x0, local copies, waits for them, and re-layouts: 3.9 us -> none  [the longest x2 3.89 us: shards(): coarse_inverse.reshape(12, DEV, 12).transpose(0, 2, 1)]
    ppermute x4, starting transfers between devices: 10.3 us -> 12.9 us  [the longest x1 5.09 us: shards(): from_right = lax.ppermute(to_left, 'member', down)]
    transpose x1 -> x0, local copies, waits for them, and re-layouts: 1.88 us -> none  [shards(): coarse_inverse.reshape(12, DEV, 12).transpose(0, 2, 1)]
  transfers between devices with their start and end apart: 5 -> 5, of which waited for: 0 -> 1; matrix products, arithmetic and copies ran while one was open for 4% -> 0% of each run, Pallas kernels for 8% -> 6%
where the time goes in v2:
time: 146 us; the launch traced here: 145 us
  blocking collectives  89.1 us (61%)
  starting transfers between devices  27.9 us (19%)
  Pallas kernels  22 us (15%)
  waiting for transfers between devices  4.17 us (3%)
    all_to_all x4, blocking collectives, exchange(): return lax.all_to_all(pay, axes, 0, 0, tiled=True)  89.1 us
    pallas_call x8, Pallas kernels, call(): pl.pallas_call(kernel, out_shape=outs, in_specs=[specs.get(i, VM) for i i...  22 us
    all_to_all x1, starting transfers between devices, exchange(): return lax.all_to_all(pay, axes, 0, 0, tiled=True)  15 us
    ppermute x1, starting transfers between devices, shards(): from_right = lax.ppermute(to_left, 'member', down)  5.09 us
    ppermute x1, starting transfers between devices, shards(): from_gm = lax.ppermute(to_gp, 'group', up)  4.57 us
    all_to_all x1, waiting for transfers between devices, exchange(): return lax.all_to_all(pay, axes, 0, 0, tiled=True)  4.16 us
  transfers between devices with their start and end apart: 5, of which 1 were waited for; matrix products, arithmetic and copies ran while one was open for 0% of the time, Pallas kernels for 6%

profile of v2, /device:TPU:1, one launch (start us, length us, event | category | flops | bytes accessed | tf_op | source)
XLA Modules:
  0.0 145.3 jit_solution(14356816616603565729)
XLA Ops:
  0.6 1.7 %shard_map.104 = (f32[2,8,768]{2,1,0:T(8,128)S(1)}, f32[256,128]{1,0:T(8,128)}) custom-call(f32[1,2,768]{2,1,0:T(2,128)} %load_hbm.3, s32[1,3,2,256]{3,2,1,0:T(2,128)} %bitcast.34), custom_call_target="tpu_custom_call" | custom-call | tf_op jit(solution)/shard_map/pallas_call | solution.py:608
  2.4 4.0 %shard_map.105 = (bf16[2,768,256]{2,1,0:T(8,128)(2,1)S(1)}, bf16[2,768,768]{2,1,0:T(8,128)(2,1)}, f32[2,16,768]{2,1,0:T(8,128)}, f32[8,768]{1,0:T(8,128)S(1)}, f...) custom-call(f32[2,8,768]{2,1,0:T(8,128)S(1)} %get-tuple-element.31.modes_ref, ...), custom_call_target="tpu_custom_call" | custom-call | tf_op jit(solution)/shard_map/pallas_call | solution.py:608
  6.3 1.3 collective-permute-start.3
  7.6 4.6 %collective-permute-start.2 = (f32[16,3200]{1,0:T(8,128)S(1)}, f32[16,3200]{1,0:T(8,128)S(1)}, u32[]{:S(2)}, u32[]{:S(2)}) collective-permute-start(f32[16,3200]{1,0:T(8,128)S(1)} %get-tuple-element.38), channel_id=1, source_target_pairs={{0,16},{16,32},{32,48},{48,64},{64,80},{80,96},{96,112},{112,128},... | collective-permute-start | bytes 614408 | tf_op jit(solution)/shard_map/ppermute | solution.py:658
  12.2 5.1 %collective-permute-start = (f32[8,3200]{1,0:T(8,128)S(1)}, f32[8,3200]{1,0:T(8,128)S(1)}, u32[]{:S(2)}, u32[]{:S(2)}) collective-permute-start(f32[8,3200]{1,0:T(8,128)S(1)} %get-tuple-element.36), channel_id=1, source_target_pairs={{1,0},{2,1},{3,2},{4,3},{5,4},{6,5},{7,6},{8,7},{9,8},{10,9},{11,1... | collective-permute-start | bytes 307208 | tf_op jit(solution)/shard_map/ppermute | solution.py:655
  17.3 1.9 %collective-permute-start.1 = (f32[8,3200]{1,0:T(8,128)S(1)}, f32[8,3200]{1,0:T(8,128)S(1)}, u32[]{:S(2)}, u32[]{:S(2)}) collective-permute-start(f32[8,3200]{1,0:T(8,128)S(1)} %get-tuple-element.37), channel_id=1, source_target_pairs={{0,1},{1,2},{2,3},{3,4},{4,5},{5,6},{6,7},{7,8},{8,9},{9,10},{10,1... | collective-permute-start | bytes 307208 | tf_op jit(solution)/shard_map/ppermute | solution.py:656
  19.2 15.0 %all-to-all-start = ((f32[256,1,128]{2,1,0:T(1,128)}), f32[256,1,128]{2,1,0:T(1,128)S(1)}, u32[]{:S(2)}, u32[]{:S(2)}) async-start(f32[256,1,128]{2,1,0:T(1,128)} %bitcast.2), calls=%async_computation | async-start | bytes 262144 | tf_op jit(solution)/shard_map/all_to_all | solution.py:636
  34.3 8.6 %shard_map.106.inv_hbm.inv_ref = f32[2,768,768]{2,1,0:T(8,128)} custom-call(f32[1,2,768,768]{3,2,1,0:T(8,128)} %l_hbm.1), custom_call_target="tpu_custom_call" | custom-call | flops 20000000000 | bytes 1048576 | tf_op jit(solution)/shard_map/pallas_call | solution.py:608
  42.9 0.0 slice-start
  42.9 0.0 collective-permute-done
  42.9 0.0 collective-permute-done.1
  42.9 0.0 collective-permute-done.3
  42.9 0.0 collective-permute-done.2
  43.0 4.2 %all-to-all-done = f32[256,1,128]{2,1,0:T(1,128)S(1)} async-done(((f32[256,1,128]{2,1,0:T(1,128)}), f32[256,1,128]{2,1,0:T(1,128)S(1)}, u32[]{:S(2)}, u32[]{:S(2)}) %all-to-all-start) | async-done | bytes 131104 | tf_op jit(solution)/shard_map/all_to_all | solution.py:636
  47.1 0.0 slice-start.1
  47.1 2.8 %shard_map.107 = (f32[2,40,768]{2,1,0:T(8,128)S(1)}, f32[64,3072]{1,0:T(8,128)S(1)}, f32[12,768]{1,0:T(8,128)S(1)}, f32[2,256]{1,0:T(2,128)S(1)}, f32[256,256]{1,0:T(8,128)S(1)}) custom-call(f32[256,128]{1,0:T(8,128)S(1)} %bitcast.29, bf16[2,768,256]{2,1,0:T(8,128)(2,1)S(1)} %get-tuple-element.32.tt_ref, f32[8,768]{1,0:T(8,128)S(1)} %get-tuple-element.33.aux_ref, ...), custom_call_target="tpu_custom_call" | custom-call | tf_op jit(solution)/shard_map/pallas_call | solution.py:608
  49.9 0.3 copy.12
  50.2 25.3 %all_to_all.55 = f32[256,1,256]{2,1,0:T(1,128)S(1)} all-to-all(f32[256,1,256]{2,1,0:T(1,128)S(1)} %copy.12), channel_id=1, replica_groups=mesh['group'=16,'member'=16] {'group','member'}, dimensions={0} | all-to-all | bytes 524288 | tf_op jit(solution)/shard_map/all_to_all | solution.py:636
  75.5 0.0 slice-done
  75.5 0.0 slice-done.1
  75.5 1.1 shard_map.108
  76.6 0.3 copy.13
  76.9 21.2 %all_to_all.56 = f32[256,1,256]{2,1,0:T(1,128)S(1)} all-to-all(f32[256,1,256]{2,1,0:T(1,128)S(1)} %copy.13), channel_id=1, replica_groups=mesh['group'=16,'member'=16] {'group','member'}, dimensions={0} | all-to-all | bytes 524288 | tf_op jit(solution)/shard_map/all_to_all | solution.py:636
  98.2 1.1 shard_map.109
  99.3 0.3 copy.14
  99.6 0.0 copy-start
  99.6 21.4 %all_to_all.57 = f32[256,1,256]{2,1,0:T(1,128)S(1)} all-to-all(f32[256,1,256]{2,1,0:T(1,128)S(1)} %copy.14), channel_id=1, replica_groups=mesh['group'=16,'member'=16] {'group','member'}, dimensions={0} | all-to-all | bytes 524288 | tf_op jit(solution)/shard_map/all_to_all | solution.py:636
  121.0 1.2 shard_map.110
  122.2 0.3 copy.15
  122.5 21.2 %all_to_all.58 = f32[256,1,256]{2,1,0:T(1,128)S(1)} all-to-all(f32[256,1,256]{2,1,0:T(1,128)S(1)} %copy.15), channel_id=1, replica_groups=mesh['group'=16,'member'=16] {'group','member'}, dimensions={0} | all-to-all | bytes 524288 | tf_op jit(solution)/shard_map/all_to_all | solution.py:636
  143.7 0.0 copy-done
  143.7 1.5 %shard_map.111 = (f32[2,768]{1,0:T(2,128)}, f32[2,768]{1,0:T(2,128)}) custom-call(f32[256,256]{1,0:T(8,128)S(1)} %bitcast.25, f32[12,768]{1,0:T(8,128)S(1)} %get-tuple-element.52.st_ref, f32[2,256]{1,0:T(2,128)S(1)} %get-tuple-element.53.o_ref, f32[24,256]{1,0:T(8,128)S(1)} %get-tuple-element.54.hs_ref, bf16[2,768,256]{2,1,0:T(8,128)(2,1)S(1)} %get-tuple-element.32.tt_ref, ...), custom_call_target="tpu_custom_call" | custom-call | tf_op jit(solution)/shard_map/pallas_call | solution.py:608
  (7 shorter events, 0.1 us)
Async XLA Ops:
  6.3 36.6 %collective-permute-start.3 = (f32[16,3200]{1,0:T(8,128)S(1)}, f32[16,3200]{1,0:T(8,128)S(1)}, u32[]{:S(2)}, u32[]{:S(2)}) collective-permute-start(f32[16,3200]{1,0:T(8,128)S(1)} %get-tuple-element.35.mine_ref), channel_id=1, source_target_pairs={{16,0},{32,16},{48,32},{64,48},{80,64},{96,80},{112,96},{128,112},... | collective-permute-start | bytes 614408 | tf_op jit(solution)/shard_map/ppermute | solution.py:657
  7.6 35.3 %collective-permute-start.2 = (f32[16,3200]{1,0:T(8,128)S(1)}, f32[16,3200]{1,0:T(8,128)S(1)}, u32[]{:S(2)}, u32[]{:S(2)}) collective-permute-start(f32[16,3200]{1,0:T(8,128)S(1)} %get-tuple-element.38), channel_id=1, source_target_pairs={{0,16},{16,32},{32,48},{48,64},{64,80},{80,96},{96,112},{112,128},... | collective-permute-start | bytes 614408 | tf_op jit(solution)/shard_map/ppermute | solution.py:658
  12.2 30.7 %collective-permute-start = (f32[8,3200]{1,0:T(8,128)S(1)}, f32[8,3200]{1,0:T(8,128)S(1)}, u32[]{:S(2)}, u32[]{:S(2)}) collective-permute-start(f32[8,3200]{1,0:T(8,128)S(1)} %get-tuple-element.36), channel_id=1, source_target_pairs={{1,0},{2,1},{3,2},{4,3},{5,4},{6,5},{7,6},{8,7},{9,8},{10,9},{11,1... | collective-permute-start | bytes 307208 | tf_op jit(solution)/shard_map/ppermute | solution.py:655
  17.3 25.6 %collective-permute-start.1 = (f32[8,3200]{1,0:T(8,128)S(1)}, f32[8,3200]{1,0:T(8,128)S(1)}, u32[]{:S(2)}, u32[]{:S(2)}) collective-permute-start(f32[8,3200]{1,0:T(8,128)S(1)} %get-tuple-element.37), channel_id=1, source_target_pairs={{0,1},{1,2},{2,3},{3,4},{4,5},{5,6},{6,7},{7,8},{8,9},{9,10},{10,1... | collective-permute-start | bytes 307208 | tf_op jit(solution)/shard_map/ppermute | solution.py:656
  19.2 27.9 %all-to-all-start = ((f32[256,1,128]{2,1,0:T(1,128)}), f32[256,1,128]{2,1,0:T(1,128)S(1)}, u32[]{:S(2)}, u32[]{:S(2)}) async-start(f32[256,1,128]{2,1,0:T(1,128)} %bitcast.2), calls=%async_computation | async-start | bytes 262144 | tf_op jit(solution)/shard_map/all_to_all | solution.py:636
  42.9 32.6 %slice-start = ((s8[4718592]{0:T(1024)(128)(4,1)}), s8[524288]{0:T(1024)(128)(4,1)S(1)}, s32[]{:S(2)}) async-start(s8[4718592]{0:T(1024)(128)(4,1)} %bitcast.23), calls=%async_computation.5 | async-start | bytes 1048576
  47.1 28.4 %slice-start.1 = ((s8[4718592]{0:T(1024)(128)(4,1)}), s8[4194304]{0:T(1024)(128)(4,1)S(1)}, s32[]{:S(2)}) async-start(s8[4718592]{0:T(1024)(128)(4,1)} %bitcast.23), calls=%async_computation.6 | async-start | bytes 8388608
  99.6 44.1 %copy-start = (bf16[2,768,768]{2,1,0:T(8,128)(2,1)S(1)}, bf16[2,768,768]{2,1,0:T(8,128)(2,1)}, u32[]{:S(2)}) copy-start(bf16[2,768,768]{2,1,0:T(8,128)(2,1)} %get-tuple-element.55.qt_ref) | copy-start | bytes 7077892

commit v3 on v2

--- a/solution.py
+++ b/solution.py
@@ -63,9 +63,9 @@
 
 
 def tables_kernel(
-    modes_ref, load_hbm, map_hbm, sign_hbm, live_hbm, slot_hbm, count_hbm, coarse_hbm,
-    tt_ref, qt_hbm, own_hbm, aux_ref, left_ref, right_ref, gm_ref, gp_ref,
-    load_ref, map_ref, sign_ref, live_ref, slot_ref, count_ref, coarse_ref, own_ref, qt_ref, sems,
+    modes_ref, load_hbm, map_hbm, sign_hbm, live_hbm, slot_hbm, count_hbm, coarse_hbm, l_hbm,
+    tt_ref, qt_hbm, own_hbm, aux_ref, sib_ref, far_ref, g1_ref, g2_ref, d_ref,
+    load_ref, map_ref, sign_ref, live_ref, slot_ref, count_ref, coarse_ref, own_ref, qt_ref, sems, sems_d,
 ):
     copies = [
         pltpu.make_async_copy(src, dst, sems.at[i])
@@ -78,6 +78,15 @@
         )
     ]
     for c in copies:
+        c.start()
+    blocks = [
+        pltpu.make_async_copy(
+            l_hbm.at[0, s, pl.ds(b * LN, LN), pl.ds(b * LN, LN)], d_ref.at[s * NCH + b], sems_d.at[s * NCH + b]
+        )
+        for s in range(2)
+        for b in range(NCH)
+    ]
+    for c in blocks:
         c.start()
     part = iota((8, ND), 0)
     for c in copies[:-1]:
@@ -130,13 +139,15 @@
         faces.append(face)
     wide = 12 * DEV
     to_left, to_right, to_gm, to_gp = pack_faces(faces[0], faces[1])
-    left_ref[:, wide:] = to_left
-    right_ref[:, wide:] = to_right
+    even_m = lax.axis_index("member") % 2 == 0
+    even_g = lax.axis_index("group") % 2 == 0
+    sib_ref[:, wide:] = jnp.where(even_m, to_right, to_left)
+    far_ref[:, wide:] = jnp.where(even_m, to_left, to_right)
     zero = jnp.zeros((8, LN), F32)
-    gm_ref[0:8, wide:] = to_gm
-    gp_ref[0:8, wide:] = to_gp
-    gm_ref[8:16, wide:] = zero
-    gp_ref[8:16, wide:] = zero
+    g1_ref[0:8, wide:] = jnp.where(even_g, to_gp, to_gm)
+    g2_ref[0:8, wide:] = jnp.where(even_g, to_gm, to_gp)
+    g1_ref[8:16, wide:] = zero
+    g2_ref[8:16, wide:] = zero
     own_copy = pltpu.make_async_copy(own_ref, own_hbm, sems.at[7])
     own_copy.start()
     late.append(own_copy)
@@ -168,11 +179,11 @@
                 src = pltpu.roll(src, shift, 1) if shift else src
                 acc = src if acc is None else jnp.where(quarter == i, src, acc)
             at = v * DEV + half * LN
-            left_ref[:, at : at + LN] = acc[0:8]
-            right_ref[:, at : at + LN] = acc[8:16]
-            gm_ref[:, at : at + LN] = acc
-            gp_ref[:, at : at + LN] = acc
-    for c in late:
+            sib_ref[:, at : at + LN] = jnp.where(even_m, acc[8:16], acc[0:8])
+            far_ref[:, at : at + LN] = jnp.where(even_m, acc[0:8], acc[8:16])
+            g1_ref[:, at : at + LN] = acc
+            g2_ref[:, at : at + LN] = acc
+    for c in late + blocks:
         c.wait()
 
 
@@ -233,19 +244,16 @@
     return d(ah, bh) + (d(ah, bl) + d(al, bh))
 
 
-def invert_kernel(l_hbm,out_hbm,out_ref,l_ref,d_ref,x_ref,sem_d,sem_l,sem_o):
-    copies_d=[pltpu.make_async_copy(l_hbm.at[0,s,pl.ds(b*LN,LN),pl.ds(b*LN,LN)],d_ref.at[s*NCH+b],sem_d.at[s*NCH+b]) for s in range(2) for b in range(NCH)]
-    for c in copies_d: c.start()
+def invert_kernel(l_hbm,diag_ref,out_hbm,out_ref,l_ref,d_ref,x_ref,sem_l,sem_o):
     copies_l=[pltpu.make_async_copy(l_hbm.at[0,s,pl.ds(b*LN,LN),pl.ds(0,b*LN)],l_ref.at[s,pl.ds(b*LN,LN),pl.ds(0,b*LN)],sem_l.at[s*NCH+b]) for s in range(2) for b in range(1,NCH)]
     for c in copies_l: c.start()
     ri=iota((LN,LN),0); ci=iota((LN,LN),1); eye=ri==ci; below=ri>ci
     lane=iota((BASE,LN),1); row=iota((BASE,LN),0)
     nb=2*NCH; ng=LN//BASE
     group=(lane//BASE)*BASE
-    for c in copies_d: c.wait()
     packs=[]
     for k in range(nb):
-        lb=d_ref[k]
+        lb=diag_ref[k]
         diag=jnp.sum(jnp.where(eye,lb,0.0),axis=1,keepdims=True)
         n=jnp.where(below,lb*(1.0/diag),0.0)
         rowdiag=jnp.sum(jnp.where(eye,lb,0.0),axis=0,keepdims=True)
@@ -360,14 +368,16 @@
 
 
 def received_coarse(recv_ref):
-    xt = jnp.transpose(recv_ref[:, 0:LN])
+    xt = jnp.transpose(recv_ref[...])
 
     def grp(i):
         return xt[8 * i : 8 * i + 8, :]
 
     h0 = grp(0) + pltpu.roll(grp(2), 1, 1) + pltpu.roll(grp(4), DEV - 16, 1) + pltpu.roll(grp(6), 16, 1)
     h1 = grp(1) + pltpu.roll(grp(3), DEV - 1, 1) + pltpu.roll(grp(5), DEV - 16, 1) + pltpu.roll(grp(7), 16, 1)
-    sums = jnp.sum(grp(8), axis=1, keepdims=True)
+    sums = jnp.concatenate(
+        [jnp.sum(grp(i), axis=1, keepdims=True)[6:8] for i in range(2)], axis=0
+    )
     return h0, h1, sums
 
 
@@ -393,11 +403,14 @@
     g = lax.axis_index("group")
     m = lax.axis_index("member")
     me = g * 16 + m
+    sib = me + 1 - 2 * (m % 2)
     return (
         jnp.where(m > 0, me - 1, me),
         jnp.where(m < 15, me + 1, me),
         jnp.where(g > 0, me - 16, me),
         jnp.where(g < 15, me + 16, me),
+        jnp.where(g > 0, sib - 16, me),
+        jnp.where(g < 15, sib + 16, me),
     )
 
 
@@ -408,19 +421,19 @@
 
 def face_row(recv_ref, row):
     base, offset = tile_of(row)
-    tile = recv_ref[pl.ds(base, 8), LN : 2 * LN]
+    tile = recv_ref[pl.ds(base, 8), :]
     return jnp.sum(jnp.where(iota((8, LN), 0) == offset, tile, 0.0), axis=0, keepdims=True)
 
 
 def assembled(recv_ref, y, o, tt_ref):
     lo = half_masks(1)
-    left, right, gm, gp = (face_row(recv_ref, row) for row in places())
+    left, right, gm, gp, sgm, sgp = (face_row(recv_ref, row) for row in places())
     o0l, o1l = o[0][:, :LN], o[1][:, :LN]
     in0 = jnp.concatenate(
-        [pltpu.roll(jnp.where(lo, o1l, left), 64, 1), jnp.where(lo, gm, pltpu.roll(gp, 64, 1))], axis=1
+        [pltpu.roll(jnp.where(lo, o1l, left), 64, 1), jnp.where(lo, pltpu.roll(gm, 64, 1), gp)], axis=1
     )
     in1 = jnp.concatenate(
-        [pltpu.roll(jnp.where(lo, right, o0l), 64, 1), jnp.where(lo, pltpu.roll(gm, 64, 1), gp)], axis=1
+        [jnp.where(lo, pltpu.roll(o0l, 64, 1), right), jnp.where(lo, pltpu.roll(sgm, 64, 1), sgp)], axis=1
     )
     out = []
     for s, inc in ((0, in0), (1, in1)):
@@ -429,7 +442,7 @@
     return out
 
 
-def send(pay_ref, y, tt_ref, ar_ref, dots):
+def send(row_ref, y, tt_ref, ar_ref, dots):
     o = []
     cols = []
     for s in range(2):
@@ -451,16 +464,22 @@
     diag = iota((64, LN), 0) == iota((64, LN), 1)
     row = jnp.sum(jnp.where(diag, cc, 0.0), axis=0, keepdims=True)
     lane = iota((1, LN), 1)
-    for i, value in enumerate(dots):
-        row = jnp.where(lane == 64 + i, value, row)
-    pay_ref[:, 0:LN] = jnp.broadcast_to(row, (DEV, LN))
-    pay_ref[:, LN : 2 * LN] = jnp.zeros((DEV, LN), F32)
-    to_left, to_right, to_gm, to_gp = pack_faces(o[0], o[1])
-    for row, face in zip(places(), (to_left, to_right, to_gm, to_gp)):
+    for at, value in zip((6, 7, 14, 15), dots):
+        row = jnp.where(lane == at, value, row)
+    row_ref[...] = jnp.concatenate([row, o[1][:, LN:], jnp.zeros((6, LN), F32)], axis=0)
+    return o
+
+
+def pay_kernel(row_ref, sib_ref, o_ref, pay_ref):
+    pay_ref[...] = jnp.broadcast_to(row_ref[0:1, :], (DEV, LN))
+    o0l, o0h, o1l = o_ref[0:1, 0:LN], o_ref[0:1, LN : 2 * LN], o_ref[1:2, 0:LN]
+    other = sib_ref[1:2, :]
+    faces = (pltpu.roll(o0l, 64, 1), o1l, pltpu.roll(o0h, 64, 1), o0h, pltpu.roll(other, 64, 1), other)
+    for row, face in zip(places(), faces):
         base, offset = tile_of(row)
-        old = pay_ref[pl.ds(base, 8), LN : 2 * LN]
-        pay_ref[pl.ds(base, 8), LN : 2 * LN] = jnp.where(iota((8, LN), 0) == offset, face, old)
-    return o
+        old = pay_ref[pl.ds(base, 8), :]
+        put_here = (iota((8, LN), 0) == offset) & (iota((8, LN), 1) >= 64)
+        pay_ref[pl.ds(base, 8), :] = jnp.where(put_here, face, old)
 
 
 def inner(a, b):
@@ -481,7 +500,7 @@
 
 def begin_kernel(
     recv_ref, tt_ref, aux_ref, inv_hbm, own_hbm, mine_ref, near_ref,
-    ar_ref, m_ref, st_ref, o_ref, pay_ref, inv_ref, own_ref, sems, sems_inv,
+    ar_ref, m_ref, st_ref, o_ref, row_ref, inv_ref, own_ref, sems, sems_inv,
 ):
     wide = 12 * DEV
     own_copy = pltpu.make_async_copy(own_hbm, own_ref, sems.at[0])
@@ -499,9 +518,20 @@
         c.start()
     h0, h1, _ = received_coarse(recv_ref)
     m_ref[0:16, :] = mine_ref[:, 0:wide]
-    m_ref[16:64, :] = near_ref[:, 0:wide]
+    even_m = lax.axis_index("member") % 2 == 0
+    even_g = lax.axis_index("group") % 2 == 0
+    sib, far = near_ref[0:8, :], near_ref[8:16, :]
+    first, second = near_ref[16:32, :], near_ref[32:48, :]
+    right = jnp.where(even_m, sib, far)
+    left = jnp.where(even_m, far, sib)
+    gm = jnp.where(even_g, second, first)
+    gp = jnp.where(even_g, first, second)
+    m_ref[16:24, :] = right[:, 0:wide]
+    m_ref[24:32, :] = left[:, 0:wide]
+    m_ref[32:48, :] = gm[:, 0:wide]
+    m_ref[48:64, :] = gp[:, 0:wide]
     own_copy.wait()
-    near = [near_ref[at : at + 8, wide:] for at in (8, 0, 16, 32)]
+    near = [left[:, wide:], right[:, wide:], gm[0:8, wide:], gp[0:8, wide:]]
     spread(near, own_ref, tt_ref, ar_ref)
     lam = project_rows(h0, h1, m_ref, ar_ref)
     mask = pair(aux_ref, 0)
@@ -509,13 +539,13 @@
     for c in parts:
         c.wait()
     y = [mask[s] * solve(inv_ref, s, load[s] - lam[s]) for s in range(2)]
-    o = send(pay_ref, y, tt_ref, ar_ref, [])
+    o = send(row_ref, y, tt_ref, ar_ref, [])
     put(st_ref, LAM, lam)
     put(st_ref, YV, y)
     put(o_ref, 0, o)
 
 
-def next_solve(pay_ref, inv_ref, tt_ref, ar_ref, aux_ref, p, d, yd):
+def next_solve(row_ref, inv_ref, tt_ref, ar_ref, aux_ref, p, d, yd):
     mask = pair(aux_ref, 0)
     weight = pair(aux_ref, 2)
     y = [mask[s] * solve(inv_ref, s, p[s]) for s in range(2)]
@@ -523,16 +553,16 @@
     dots = [inner(wp, p), inner(p, y)]
     if d is not None:
         dots += [inner(d, y), inner(p, yd)]
-    o = send(pay_ref, y, tt_ref, ar_ref, dots)
+    o = send(row_ref, y, tt_ref, ar_ref, dots)
     return y, o
 
 
-def first_kernel(recv_ref, st_ref, o_ref, inv_ref, tt_ref, ar_ref, m_ref, aux_ref, st2_ref, o2_ref, pay_ref):
+def first_kernel(recv_ref, st_ref, o_ref, inv_ref, tt_ref, ar_ref, m_ref, aux_ref, st2_ref, o2_ref, row_ref):
     h0, h1, _ = received_coarse(recv_ref)
     w = project_rows(h0, h1, m_ref, ar_ref)
     res = assembled(recv_ref, pair(st_ref, YV), pair(o_ref, 0), tt_ref)
     p = [res[s] - w[s] for s in range(2)]
-    y, o = next_solve(pay_ref, inv_ref, tt_ref, ar_ref, aux_ref, p, None, None)
+    y, o = next_solve(row_ref, inv_ref, tt_ref, ar_ref, aux_ref, p, None, None)
     put(st2_ref, LAM, pair(st_ref, LAM))
     put(st2_ref, PV, p)
     put(st2_ref, YV, y)
@@ -567,12 +597,12 @@
 def make_step(it):
     def step_kernel(
         recv_ref, st_ref, o_ref, hs_ref, inv_ref, tt_ref, ar_ref, m_ref, aux_ref,
-        st2_ref, o2_ref, hs2_ref, pay_ref,
+        st2_ref, o2_ref, hs2_ref, row_ref,
     ):
         lam, pn, d, yd, image, h0, h1, norm, curve = step_body(
             it, recv_ref, st_ref, o_ref, hs_ref, tt_ref, ar_ref, m_ref
         )
-        y, o = next_solve(pay_ref, inv_ref, tt_ref, ar_ref, aux_ref, pn, d, yd)
+        y, o = next_solve(row_ref, inv_ref, tt_ref, ar_ref, aux_ref, pn, d, yd)
         for at, v in ((LAM, lam), (PV, pn), (DV, d), (IM, image), (YD, yd), (YV, y)):
             put(st2_ref, at, v)
         put(o2_ref, 0, o)
@@ -637,60 +667,65 @@
 
     recv0 = exchange(pay0)
     raw = (load, dof_map, dof_sign, live_count, face_slot, face_count, coarse_inverse)
-    tt, qt, own, aux, to_left, to_right, to_gm, to_gp = call(
+    tt, qt, own, aux, to_sib, to_far, to_g1, to_g2, diag = call(
         tables_kernel,
         (
             sds((2, ND, 256), BF), pltpu.HBM((2, ND, ND), BF), pltpu.HBM((2, 16, ND), F32), sds((8, ND)),
-            sds((8, packed)), sds((8, packed)), sds((16, packed)), sds((16, packed)),
+            sds((8, packed)), sds((8, packed)), sds((16, packed)), sds((16, packed)), sds((2 * NCH, LN, LN)),
         ),
-        {i: HB for i in range(1, 8)},
-        modes, *raw,
+        {i: HB for i in range(1, 9)},
+        modes, *raw, factor,
         scratch=[pltpu.VMEM(r.shape, r.dtype) for r in raw]
-        + [pltpu.VMEM((2, 16, ND), F32), pltpu.VMEM((2, ND, ND), BF), pltpu.SemaphoreType.DMA((10,))],
+        + [pltpu.VMEM((2, 16, ND), F32), pltpu.VMEM((2, ND, ND), BF), pltpu.SemaphoreType.DMA((10,)), pltpu.SemaphoreType.DMA((2 * NCH,))],
         hbm_outs=(1, 2),
     )
 
-    up = [(i, i + 1) for i in range(15)]
-    down = [(i + 1, i) for i in range(15)]
-    from_right = lax.ppermute(to_left, "member", down)
-    from_left = lax.ppermute(to_right, "member", up)
-    from_gp = lax.ppermute(to_gm, "group", down)
-    from_gm = lax.ppermute(to_gp, "group", up)
+    swap = [(i, i ^ 1) for i in range(16)]
+    cross = [(i, ((i + 1) ^ 1) - 1) for i in range(1, 15)]
+    from_g1 = lax.ppermute(to_g1, "group", swap)
+    from_g2 = lax.ppermute(to_g2, "group", cross)
+    from_far = lax.ppermute(to_far, "member", cross)
+    from_sib = lax.ppermute(to_sib, "member", swap)
     (inv,) = call(
         invert_kernel,
         (pltpu.HBM((2, ND, ND), F32),),
         {0: HB},
-        factor,
+        factor, diag,
         scratch=[
             pltpu.VMEM((2, ND, ND), F32), pltpu.VMEM((2, ND, ND), F32), pltpu.VMEM((2 * NCH, LN, LN), F32),
             pltpu.VMEM((2 * NCH, LN, LN), F32), pltpu.SemaphoreType.DMA((2 * NCH,)),
-            pltpu.SemaphoreType.DMA((2 * NCH,)), pltpu.SemaphoreType.DMA((2 * NCH,)),
+            pltpu.SemaphoreType.DMA((2 * NCH,)),
         ],
         hbm_outs=(0,),
         flops=20_000_000_000,
         mib=24,
     )
-    near = jnp.concatenate([from_right, from_left, from_gm, from_gp], axis=0)
-    st_s, o_s, hs_s, pay_s = sds((12, ND)), sds((2, 256)), sds((24, DEV)), sds((DEV, 2 * LN))
-    ar, table, st, o, pay = call(
-        begin_kernel, (sds((2, 40, ND)), sds((64, 12 * DEV)), st_s, o_s, pay_s),
+    near = jnp.concatenate([from_sib, from_far, from_g1, from_g2], axis=0)
+    st_s, o_s, hs_s, row_s = sds((12, ND)), sds((2, 256)), sds((24, DEV)), sds((8, LN))
+
+    def gather(row, o):
+        (pay,) = call(pay_kernel, (sds((DEV, LN)),), {}, row, lax.ppermute(row, "member", swap), o)
+        return exchange(pay)
+
+    ar, table, st, o, row = call(
+        begin_kernel, (sds((2, 40, ND)), sds((64, 12 * DEV)), st_s, o_s, row_s),
         {3: HB, 4: HB},
-        recv0, tt, aux, inv, own, to_gm, near,
+        recv0, tt, aux, inv, own, to_g1, near,
         scratch=[
             pltpu.VMEM((2, ND, ND), F32), pltpu.VMEM((2, 16, ND), F32),
             pltpu.SemaphoreType.DMA((1,)), pltpu.SemaphoreType.DMA((2 * NCH,)),
         ],
     )
-    st, o, pay = call(first_kernel, (st_s, o_s, pay_s), {}, exchange(pay), st, o, inv, tt, ar, table, aux)
+    st, o, row = call(first_kernel, (st_s, o_s, row_s), {}, gather(row, o), st, o, inv, tt, ar, table, aux)
     hs = jnp.zeros((24, DEV), F32)
     for it in range(ITERS - 1):
-        st, o, hs, pay = call(
-            make_step(it), (st_s, o_s, hs_s, pay_s), {},
-            exchange(pay), st, o, hs, inv, tt, ar, table, aux,
+        st, o, hs, row = call(
+            make_step(it), (st_s, o_s, hs_s, row_s), {},
+            gather(row, o), st, o, hs, inv, tt, ar, table, aux,
         )
     lam, proj = call(
         last_kernel, (sds((2, ND)), sds((2, ND))), {},
-        exchange(pay), st, o, hs, tt, ar, table, aux, qt,
+        gather(row, o), st, o, hs, tt, ar, table, aux, qt,
     )
     return lam[None], proj[None]
 

time: 146 us -> 132 us (0.904)
  blocking collectives: 89.1 us -> 74.2 us
  waiting for transfers between devices: 4.17 us -> 9.25 us
    all_to_all x4, blocking collectives: 89.1 us -> 74.2 us  [exchange(): return lax.all_to_all(pay, axes, 0, 0, tiled=True)]
    ppermute x4 -> x8, waiting for transfers between devices: 0.01 us -> 3.3 us  [the longest x4 3.29 us: gather(): lax.ppermute(row, 'member', swap)]
    all_to_all x1, waiting for transfers between devices: 4.16 us -> 5.95 us  [exchange(): return lax.all_to_all(pay, axes, 0, 0, tiled=True)]
    ppermute x4 -> x8, starting transfers between devices: 12.9 us -> 11.3 us  [the longest x4 4.07 us: gather(): lax.ppermute(row, 'member', swap)]
    pallas_call x8 -> x12, Pallas kernels: 22 us -> 21 us  [call(): pl.pallas_call(kernel, out_shape=outs, in_specs=[specs.get(i, VM) for i i...]
  transfers between devices with their start and end apart: 5 -> 9, of which waited for: 1 -> 5; matrix products, arithmetic and copies ran while one was open for 0% -> 0% of each run, Pallas kernels for 6% -> 5%
where the time goes in v3:
time: 132 us
  blocking collectives  74.2 us (56%)
  starting transfers between devices  26.9 us (20%)
  Pallas kernels  21 us (16%)
  waiting for transfers between devices  9.25 us (7%)
    all_to_all x4, blocking collectives, exchange(): return lax.all_to_all(pay, axes, 0, 0, tiled=True)  74.2 us
    pallas_call x12, Pallas kernels, call(): pl.pallas_call(kernel, out_shape=outs, in_specs=[specs.get(i, VM) for i i...  21 us
    all_to_all x1, starting transfers between devices, exchange(): return lax.all_to_all(pay, axes, 0, 0, tiled=True)  15.5 us
    all_to_all x1, waiting for transfers between devices, exchange(): return lax.all_to_all(pay, axes, 0, 0, tiled=True)  5.95 us
    ppermute x4, starting transfers between devices, gather(): lax.ppermute(row, 'member', swap)  4.07 us
    ppermute x4, waiting for transfers between devices, gather(): lax.ppermute(row, 'member', swap)  3.29 us
    ppermute x1, starting transfers between devices, shards(): from_far = lax.ppermute(to_far, 'member', cross)  3.2 us
  transfers between devices with their start and end apart: 9, of which 5 were waited for; matrix products, arithmetic and copies ran while one was open for 0% of the time, Pallas kernels for 5%

profile of v3, /device:TPU:1, one launch (start us, length us, event | category | flops | bytes accessed | tf_op | source)
XLA Modules:
  0.0 132.1 jit_solution(1868914036905422062)
XLA Ops:
  0.6 1.7 %shard_map.104 = (f32[2,8,768]{2,1,0:T(8,128)S(1)}, f32[256,128]{1,0:T(8,128)}) custom-call(f32[1,2,768]{2,1,0:T(2,128)} %load_hbm.3, s32[1,3,2,256]{3,2,1,0:T(2,128)} %bitcast.32), custom_call_target="tpu_custom_call" | custom-call | tf_op jit(solution)/shard_map/pallas_call | solution.py:638
  2.4 4.3 %shard_map.105 = (bf16[2,768,256]{2,1,0:T(8,128)(2,1)S(1)}, bf16[2,768,768]{2,1,0:T(8,128)(2,1)}, f32[2,16,768]{2,1,0:T(8,128)}, f32[8,768]{1,0:T(8,128)S(1)}, f...) custom-call(f32[2,8,768]{2,1,0:T(8,128)S(1)} %get-tuple-element.32.m, ...), custom_call_target="tpu_custom_call" | custom-call | tf_op jit(solution)/shard_map/pallas_call | solution.py:638
  6.6 2.1 %collective-permute-start.2 = (f32[16,3200]{1,0:T(8,128)S(1)}, f32[16,3200]{1,0:T(8,128)S(1)}, u32[]{:S(2)}, u32[]{:S(2)}) collective-permute-start(f32[16,3200]{1,0:T(8,128)S(1)} %get-tuple-element.37.mine_ref), channel_id=1, source_target_pairs={{0,16},{16,0},{32,48},{48,32},{64,80},{80,64},{96,112},{112,96},{1... | collective-permute-start | bytes 614408 | tf_op jit(solution)/shard_map/ppermute | solution.py:685
  8.7 0.7 collective-permute-start.3
  9.4 1.3 collective-permute-start
  10.7 3.2 %collective-permute-start.1 = (f32[8,3200]{1,0:T(8,128)S(1)}, f32[8,3200]{1,0:T(8,128)S(1)}, u32[]{:S(2)}, u32[]{:S(2)}) collective-permute-start(f32[8,3200]{1,0:T(8,128)S(1)} %get-tuple-element.39), channel_id=1, source_target_pairs={{1,2},{2,1},{3,4},{4,3},{5,6},{6,5},{7,8},{8,7},{9,10},{10,9},{11,... | collective-permute-start | bytes 307208 | tf_op jit(solution)/shard_map/ppermute | solution.py:687
  13.9 15.5 %all-to-all-start = ((f32[256,1,128]{2,1,0:T(1,128)}), f32[256,1,128]{2,1,0:T(1,128)S(1)}, u32[]{:S(2)}, u32[]{:S(2)}) async-start(f32[256,1,128]{2,1,0:T(1,128)} %bitcast.2), calls=%async_computation | async-start | bytes 262144 | tf_op jit(solution)/shard_map/all_to_all | solution.py:666
  29.5 6.8 %shard_map.106.inv_hbm.inv_ref = f32[2,768,768]{2,1,0:T(8,128)} custom-call(f32[1,2,768,768]{3,2,1,0:T(8,128)} %l_hbm.3, f32[12,128,128]{2,1,0:T(8,128)S(1)} %get-tuple-element.35.diag_ref), custom_call_target="tpu_custom_call" | custom-call | flops 20000000000 | bytes 1048576 | tf_op jit(solution)/shard_map/pallas_call | solution.py:638
  36.3 0.0 collective-permute-done
  36.3 0.1 pad_maximum_fusion.near_ref
  36.4 5.9 %all-to-all-done = f32[256,1,128]{2,1,0:T(1,128)S(1)} async-done(((f32[256,1,128]{2,1,0:T(1,128)}), f32[256,1,128]{2,1,0:T(1,128)S(1)}, u32[]{:S(2)}, u32[]{:S(2)}) %all-to-all-start) | async-done | bytes 131104 | tf_op jit(solution)/shard_map/all_to_all | solution.py:666
  42.3 3.0 %shard_map.107 = (f32[2,40,768]{2,1,0:T(8,128)S(1)}, f32[64,3072]{1,0:T(8,128)S(1)}, f32[12,768]{1,0:T(8,128)S(1)}, f32[2,256]{1,0:T(2,128)S(1)}, f32[8,128]{1,0:T(8,128)S(1)}) custom-call(f32[256,128]{1,0:T(8,128)S(1)} %bitcast.23, bf16[2,768,256]{2,1,0:T(8,128)(2,1)S(1)} %get-tuple-element.33.tt_ref, f32[8,768]{1,0:T(8,128)S(1)} %get-tuple-element.34.aux_ref, ...), custom_call_target="tpu_custom_call" | custom-call | tf_op jit(solution)/shard_map/pallas_call | solution.py:638
  45.3 1.2 collective-permute-start.4
  46.5 0.8 collective-permute-done.4.sib_ref
  47.3 0.1 shard_map.108
  47.4 19.9 %all_to_all.55 = f32[256,1,128]{2,1,0:T(1,128)S(1)} all-to-all(f32[256,1,128]{2,1,0:T(1,128)S(1)} %bitcast.28), channel_id=1, replica_groups=mesh['group'=16,'member'=16] {'group','member'}, dimensions={0} | all-to-all | bytes 262144 | tf_op jit(solution)/shard_map/all_to_all | solution.py:666
  67.3 1.1 shard_map.109
  68.4 1.0 collective-permute-start.5
  69.4 0.8 collective-permute-done.5.sib_ref
  70.2 0.1 shard_map.110
  70.3 18.1 %all_to_all.56 = f32[256,1,128]{2,1,0:T(1,128)S(1)} all-to-all(f32[256,1,128]{2,1,0:T(1,128)S(1)} %bitcast.29), channel_id=1, replica_groups=mesh['group'=16,'member'=16] {'group','member'}, dimensions={0} | all-to-all | bytes 262144 | tf_op jit(solution)/shard_map/all_to_all | solution.py:666
  88.4 1.1 shard_map.111
  89.5 1.0 collective-permute-start.6
  90.5 0.8 collective-permute-done.6.sib_ref
  91.3 0.1 shard_map.112
  91.4 18.1 %all_to_all.57 = f32[256,1,128]{2,1,0:T(1,128)S(1)} all-to-all(f32[256,1,128]{2,1,0:T(1,128)S(1)} %bitcast.30), channel_id=1, replica_groups=mesh['group'=16,'member'=16] {'group','member'}, dimensions={0} | all-to-all | bytes 262144 | tf_op jit(solution)/shard_map/all_to_all | solution.py:666
  109.4 1.1 shard_map.113
  110.6 1.0 collective-permute-start.7
  111.6 0.8 collective-permute-done.7.sib_ref
  112.4 0.1 shard_map.114
  112.5 18.1 %all_to_all.58 = f32[256,1,128]{2,1,0:T(1,128)S(1)} all-to-all(f32[256,1,128]{2,1,0:T(1,128)S(1)} %bitcast.31), channel_id=1, replica_groups=mesh['group'=16,'member'=16] {'group','member'}, dimensions={0} | all-to-all | bytes 262144 | tf_op jit(solution)/shard_map/all_to_all | solution.py:666
  130.6 1.5 %shard_map.115 = (f32[2,768]{1,0:T(2,128)}, f32[2,768]{1,0:T(2,128)}) custom-call(f32[256,128]{1,0:T(8,128)S(1)} %bitcast.24, f32[12,768]{1,0:T(8,128)S(1)} %get-tuple-element.55.st_ref, f32[2,256]{1,0:T(2,128)S(1)} %get-tuple-element.54.o_ref, f32[24,256]{1,0:T(8,128)S(1)} %get-tuple-element.56.hs_ref, bf16[2,768,256]{2,1,0:T(8,128)(2,1)S(1)} %get-tuple-element.33.tt_ref, ...), custom_call_target="tpu_custom_call" | custom-call | tf_op jit(solution)/shard_map/pallas_call | solution.py:638
  (8 shorter events, 0.0 us)
Async XLA Ops:
  6.6 29.7 %collective-permute-start.2 = (f32[16,3200]{1,0:T(8,128)S(1)}, f32[16,3200]{1,0:T(8,128)S(1)}, u32[]{:S(2)}, u32[]{:S(2)}) collective-permute-start(f32[16,3200]{1,0:T(8,128)S(1)} %get-tuple-element.37.mine_ref), channel_id=1, source_target_pairs={{0,16},{16,0},{32,48},{48,32},{64,80},{80,64},{96,112},{112,96},{1... | collective-permute-start | bytes 614408 | tf_op jit(solution)/shard_map/ppermute | solution.py:685
  8.7 27.6 %collective-permute-start.3 = (f32[16,3200]{1,0:T(8,128)S(1)}, f32[16,3200]{1,0:T(8,128)S(1)}, u32[]{:S(2)}, u32[]{:S(2)}) collective-permute-start(f32[16,3200]{1,0:T(8,128)S(1)} %get-tuple-element.40), channel_id=1, source_target_pairs={{16,32},{32,16},{48,64},{64,48},{80,96},{96,80},{112,128},{128,112... | collective-permute-start | bytes 614408 | tf_op jit(solution)/shard_map/ppermute | solution.py:686
  9.4 26.9 %collective-permute-start = (f32[8,3200]{1,0:T(8,128)S(1)}, f32[8,3200]{1,0:T(8,128)S(1)}, u32[]{:S(2)}, u32[]{:S(2)}) collective-permute-start(f32[8,3200]{1,0:T(8,128)S(1)} %get-tuple-element.38), channel_id=1, source_target_pairs={{0,1},{1,0},{2,3},{3,2},{4,5},{5,4},{6,7},{7,6},{8,9},{9,8},{10,11... | collective-permute-start | bytes 307208 | tf_op jit(solution)/shard_map/ppermute | solution.py:688
  10.7 25.6 %collective-permute-start.1 = (f32[8,3200]{1,0:T(8,128)S(1)}, f32[8,3200]{1,0:T(8,128)S(1)}, u32[]{:S(2)}, u32[]{:S(2)}) collective-permute-start(f32[8,3200]{1,0:T(8,128)S(1)} %get-tuple-element.39), channel_id=1, source_target_pairs={{1,2},{2,1},{3,4},{4,3},{5,6},{6,5},{7,8},{8,7},{9,10},{10,9},{11,... | collective-permute-start | bytes 307208 | tf_op jit(solution)/shard_map/ppermute | solution.py:687
  13.9 28.4 %all-to-all-start = ((f32[256,1,128]{2,1,0:T(1,128)}), f32[256,1,128]{2,1,0:T(1,128)S(1)}, u32[]{:S(2)}, u32[]{:S(2)}) async-start(f32[256,1,128]{2,1,0:T(1,128)} %bitcast.2), calls=%async_computation | async-start | bytes 262144 | tf_op jit(solution)/shard_map/all_to_all | solution.py:666
  42.3 25.0 %copy-start = (f32[2,768,768]{2,1,0:T(8,128)S(1)}, f32[2,768,768]{2,1,0:T(8,128)}, u32[]{:S(2)}) copy-start(f32[2,768,768]{2,1,0:T(8,128)} %shard_map.106.inv_hbm.inv_ref) | copy-start | bytes 14155780
  45.3 2.0 %collective-permute-start.4 = (f32[8,128]{1,0:T(8,128)S(1)}, f32[8,128]{1,0:T(8,128)S(1)}, u32[]{:S(2)}, u32[]{:S(2)}) collective-permute-start(f32[8,128]{1,0:T(8,128)S(1)} %get-tuple-element.41.row_ref), channel_id=1, source_target_pairs={{0,1},{1,0},{2,3},{3,2},{4,5},{5,4},{6,7},{7,6},{8,9},{9,8},{10,11... | collective-permute-start | bytes 12296 | tf_op jit(solution)/shard_map/ppermute | solution.py:707
  68.4 1.8 %collective-permute-start.5 = (f32[8,128]{1,0:T(8,128)S(1)}, f32[8,128]{1,0:T(8,128)S(1)}, u32[]{:S(2)}, u32[]{:S(2)}) collective-permute-start(f32[8,128]{1,0:T(8,128)S(1)} %get-tuple-element.46.row_ref), channel_id=1, source_target_pairs={{0,1},{1,0},{2,3},{3,2},{4,5},{5,4},{6,7},{7,6},{8,9},{9,8},{10,11... | collective-permute-start | bytes 12296 | tf_op jit(solution)/shard_map/ppermute | solution.py:707
  89.5 41.1 %copy-start.1 = (bf16[2,768,768]{2,1,0:T(8,128)(2,1)S(1)}, bf16[2,768,768]{2,1,0:T(8,128)(2,1)}, u32[]{:S(2)}) copy-start(bf16[2,768,768]{2,1,0:T(8,128)(2,1)} %get-tuple-element.57.qt_ref) | copy-start | bytes 7077892
  89.5 1.8 %collective-permute-start.6 = (f32[8,128]{1,0:T(8,128)S(1)}, f32[8,128]{1,0:T(8,128)S(1)}, u32[]{:S(2)}, u32[]{:S(2)}) collective-permute-start(f32[8,128]{1,0:T(8,128)S(1)} %get-tuple-element.49.row_ref), channel_id=1, source_target_pairs={{0,1},{1,0},{2,3},{3,2},{4,5},{5,4},{6,7},{7,6},{8,9},{9,8},{10,11... | collective-permute-start | bytes 12296 | tf_op jit(solution)/shard_map/ppermute | solution.py:707
  110.6 1.8 %collective-permute-start.7 = (f32[8,128]{1,0:T(8,128)S(1)}, f32[8,128]{1,0:T(8,128)S(1)}, u32[]{:S(2)}, u32[]{:S(2)}) collective-permute-start(f32[8,128]{1,0:T(8,128)S(1)} %get-tuple-element.53.row_ref), channel_id=1, source_target_pairs={{0,1},{1,0},{2,3},{3,2},{4,5},{5,4},{6,7},{7,6},{8,9},{9,8},{10,11... | collective-permute-start | bytes 12296 | tf_op jit(solution)/shard_map/ppermute | solution.py:707

commit v4 on v3

--- a/solution.py
+++ b/solution.py
@@ -20,10 +20,20 @@
     return lax.broadcasted_iota(jnp.int32, shape, dim)
 
 
-def coarse_kernel(load_hbm, node_hbm, modes_ref, pay_ref, load_ref, node_ref, sems):
+def coarse_kernel(
+    load_hbm, node_hbm, map_hbm, sign_hbm, live_hbm, slot_hbm, count_hbm, coarse_hbm,
+    modes_ref, pay_ref, load_ref, map_ref, sign_ref, live_ref, slot_ref, count_ref, coarse_ref,
+    node_ref, sems,
+):
     copies = [
-        pltpu.make_async_copy(node_hbm, node_ref, sems.at[0]),
-        pltpu.make_async_copy(load_hbm, load_ref, sems.at[1]),
+        pltpu.make_async_copy(src, dst, sems.at[i])
+        for i, (src, dst) in enumerate(
+            (
+                (node_hbm, node_ref), (load_hbm, load_ref), (map_hbm, map_ref), (sign_hbm, sign_ref),
+                (live_hbm, live_ref), (slot_hbm, slot_ref), (count_hbm, count_ref),
+                (coarse_hbm, coarse_ref),
+            )
+        )
     ]
     for c in copies:
         c.start()
@@ -39,7 +49,7 @@
     third = (comp == 2.0).astype(F32)
     delta = iota((256, ND), 1) - 3 * iota((256, ND), 0)
     rep = jnp.where((delta >= 0) & (delta < 3), 1.0, 0.0).astype(BF)
-    for c in copies:
+    for c in copies[:2]:
         c.wait()
     for s in range(2):
         position = (node_ref[0, :, s, :].astype(F32) - 8.0) * 0.125
@@ -60,25 +70,15 @@
         e = jnp.sum(modes * load_ref[0, s : s + 1, :], axis=1, keepdims=True)
         row = row + jnp.sum(jnp.where(lane8 == sub8 + 8 * s, e, 0.0), axis=0, keepdims=True)
     pay_ref[...] = jnp.broadcast_to(row, (DEV, LN))
+    for c in copies[2:]:
+        c.wait()
 
 
 def tables_kernel(
-    modes_ref, load_hbm, map_hbm, sign_hbm, live_hbm, slot_hbm, count_hbm, coarse_hbm, l_hbm,
+    modes_ref, load_ref, map_ref, sign_ref, live_ref, slot_ref, count_ref, coarse_ref, l_hbm,
     tt_ref, qt_hbm, own_hbm, aux_ref, sib_ref, far_ref, g1_ref, g2_ref, d_ref,
-    load_ref, map_ref, sign_ref, live_ref, slot_ref, count_ref, coarse_ref, own_ref, qt_ref, sems, sems_d,
+    own_ref, qt_ref, sems, sems_d,
 ):
-    copies = [
-        pltpu.make_async_copy(src, dst, sems.at[i])
-        for i, (src, dst) in enumerate(
-            (
-                (load_hbm, load_ref), (map_hbm, map_ref), (sign_hbm, sign_ref),
-                (live_hbm, live_ref), (slot_hbm, slot_ref), (count_hbm, count_ref),
-                (coarse_hbm, coarse_ref),
-            )
-        )
-    ]
-    for c in copies:
-        c.start()
     blocks = [
         pltpu.make_async_copy(
             l_hbm.at[0, s, pl.ds(b * LN, LN), pl.ds(b * LN, LN)], d_ref.at[s * NCH + b], sems_d.at[s * NCH + b]
@@ -89,8 +89,6 @@
     for c in blocks:
         c.start()
     part = iota((8, ND), 0)
-    for c in copies[:-1]:
-        c.wait()
     faces = []
     late = []
     for s in range(2):
@@ -119,7 +117,7 @@
         tt_ref[s] = tt_b
         qt = jnp.where(iota((ND, ND), 0) == dof, 1.0, 0.0).astype(BF)
         qt_ref[s] = qt
-        qt_copy = pltpu.make_async_copy(qt_ref.at[s], qt_hbm.at[s], sems.at[8 + s])
+        qt_copy = pltpu.make_async_copy(qt_ref.at[s], qt_hbm.at[s], sems.at[1 + s])
         qt_copy.start()
         late.append(qt_copy)
         mask = lax.dot_general(
@@ -148,10 +146,9 @@
     g2_ref[0:8, wide:] = jnp.where(even_g, to_gm, to_gp)
     g1_ref[8:16, wide:] = zero
     g2_ref[8:16, wide:] = zero
-    own_copy = pltpu.make_async_copy(own_ref, own_hbm, sems.at[7])
+    own_copy = pltpu.make_async_copy(own_ref, own_hbm, sems.at[0])
     own_copy.start()
     late.append(own_copy)
-    copies[-1].wait()
     perm = jnp.where(
         (iota((384, 384), 0) - 12 * (iota((384, 384), 1) % 32)) == iota((384, 384), 1) // 32, 1.0, 0.0
     ).astype(BF)
@@ -442,38 +439,50 @@
     return out
 
 
-def send(row_ref, y, tt_ref, ar_ref, dots):
+def faces_of(y, tt_ref):
     o = []
-    cols = []
     for s in range(2):
         prod = jnp.dot(split3([y[s]], 8), tt_ref[s], preferred_element_type=F32)
         o.append(jnp.sum(prod, axis=0, keepdims=True))
-        cols.append(jnp.sum(ar_ref[s] * y[s], axis=1, keepdims=True))
-    c0, c1 = cols
-
-    def grp(c, i):
-        return c[8 * i : 8 * i + 8, :]
-
-    cc = jnp.concatenate(
-        [
-            grp(c0, 0) + grp(c1, 0), grp(c0, 1) + grp(c1, 1), grp(c1, 2), grp(c0, 2),
-            grp(c0, 3), grp(c1, 3), grp(c0, 4), grp(c1, 4),
-        ],
-        axis=0,
-    )
-    diag = iota((64, LN), 0) == iota((64, LN), 1)
-    row = jnp.sum(jnp.where(diag, cc, 0.0), axis=0, keepdims=True)
-    lane = iota((1, LN), 1)
-    for at, value in zip((6, 7, 14, 15), dots):
-        row = jnp.where(lane == at, value, row)
-    row_ref[...] = jnp.concatenate([row, o[1][:, LN:], jnp.zeros((6, LN), F32)], axis=0)
     return o
+
+
+def make_coef(count):
+    def coef_kernel(st_ref, ar_ref, aux_ref, row_ref):
+        y = pair(st_ref, YV)
+        c0, c1 = (jnp.sum(ar_ref[s] * y[s], axis=1, keepdims=True) for s in range(2))
+
+        def grp(c, i):
+            return c[8 * i : 8 * i + 8, :]
+
+        cc = jnp.concatenate(
+            [
+                grp(c0, 0) + grp(c1, 0), grp(c0, 1) + grp(c1, 1), grp(c1, 2), grp(c0, 2),
+                grp(c0, 3), grp(c1, 3), grp(c0, 4), grp(c1, 4),
+            ],
+            axis=0,
+        )
+        diag = iota((64, LN), 0) == iota((64, LN), 1)
+        row = jnp.sum(jnp.where(diag, cc, 0.0), axis=0, keepdims=True)
+        lane = iota((1, LN), 1)
+        dots = []
+        if count >= 2:
+            p = pair(st_ref, PV)
+            weight = pair(aux_ref, 2)
+            dots = [inner([weight[s] * p[s] for s in range(2)], p), inner(p, y)]
+        if count >= 4:
+            dots += [inner(pair(st_ref, DV), y), inner(p, pair(st_ref, YD))]
+        for at, value in zip((6, 7, 14, 15), dots):
+            row = jnp.where(lane == at, value, row)
+        row_ref[...] = jnp.broadcast_to(row, (8, LN))
+
+    return coef_kernel
 
 
 def pay_kernel(row_ref, sib_ref, o_ref, pay_ref):
     pay_ref[...] = jnp.broadcast_to(row_ref[0:1, :], (DEV, LN))
     o0l, o0h, o1l = o_ref[0:1, 0:LN], o_ref[0:1, LN : 2 * LN], o_ref[1:2, 0:LN]
-    other = sib_ref[1:2, :]
+    other = sib_ref[1:2, LN : 2 * LN]
     faces = (pltpu.roll(o0l, 64, 1), o1l, pltpu.roll(o0h, 64, 1), o0h, pltpu.roll(other, 64, 1), other)
     for row, face in zip(places(), faces):
         base, offset = tile_of(row)
@@ -500,7 +509,7 @@
 
 def begin_kernel(
     recv_ref, tt_ref, aux_ref, inv_hbm, own_hbm, mine_ref, near_ref,
-    ar_ref, m_ref, st_ref, o_ref, row_ref, inv_ref, own_ref, sems, sems_inv,
+    ar_ref, m_ref, st_ref, o_ref, inv_ref, own_ref, sems, sems_inv,
 ):
     wide = 12 * DEV
     own_copy = pltpu.make_async_copy(own_hbm, own_ref, sems.at[0])
@@ -539,30 +548,24 @@
     for c in parts:
         c.wait()
     y = [mask[s] * solve(inv_ref, s, load[s] - lam[s]) for s in range(2)]
-    o = send(row_ref, y, tt_ref, ar_ref, [])
+    o = faces_of(y, tt_ref)
     put(st_ref, LAM, lam)
     put(st_ref, YV, y)
     put(o_ref, 0, o)
 
 
-def next_solve(row_ref, inv_ref, tt_ref, ar_ref, aux_ref, p, d, yd):
+def next_solve(inv_ref, tt_ref, aux_ref, p):
     mask = pair(aux_ref, 0)
-    weight = pair(aux_ref, 2)
     y = [mask[s] * solve(inv_ref, s, p[s]) for s in range(2)]
-    wp = [weight[s] * p[s] for s in range(2)]
-    dots = [inner(wp, p), inner(p, y)]
-    if d is not None:
-        dots += [inner(d, y), inner(p, yd)]
-    o = send(row_ref, y, tt_ref, ar_ref, dots)
-    return y, o
-
-
-def first_kernel(recv_ref, st_ref, o_ref, inv_ref, tt_ref, ar_ref, m_ref, aux_ref, st2_ref, o2_ref, row_ref):
+    return y, faces_of(y, tt_ref)
+
+
+def first_kernel(recv_ref, st_ref, o_ref, inv_ref, tt_ref, ar_ref, m_ref, aux_ref, st2_ref, o2_ref):
     h0, h1, _ = received_coarse(recv_ref)
     w = project_rows(h0, h1, m_ref, ar_ref)
     res = assembled(recv_ref, pair(st_ref, YV), pair(o_ref, 0), tt_ref)
     p = [res[s] - w[s] for s in range(2)]
-    y, o = next_solve(row_ref, inv_ref, tt_ref, ar_ref, aux_ref, p, None, None)
+    y, o = next_solve(inv_ref, tt_ref, aux_ref, p)
     put(st2_ref, LAM, pair(st_ref, LAM))
     put(st2_ref, PV, p)
     put(st2_ref, YV, y)
@@ -597,12 +600,12 @@
 def make_step(it):
     def step_kernel(
         recv_ref, st_ref, o_ref, hs_ref, inv_ref, tt_ref, ar_ref, m_ref, aux_ref,
-        st2_ref, o2_ref, hs2_ref, row_ref,
+        st2_ref, o2_ref, hs2_ref,
     ):
         lam, pn, d, yd, image, h0, h1, norm, curve = step_body(
             it, recv_ref, st_ref, o_ref, hs_ref, tt_ref, ar_ref, m_ref
         )
-        y, o = next_solve(row_ref, inv_ref, tt_ref, ar_ref, aux_ref, pn, d, yd)
+        y, o = next_solve(inv_ref, tt_ref, aux_ref, pn)
         for at, v in ((LAM, lam), (PV, pn), (DV, d), (IM, image), (YD, yd), (YV, y)):
             put(st2_ref, at, v)
         put(o2_ref, 0, o)
@@ -651,32 +654,31 @@
 def shards(factor, load, dof_map, dof_sign, live_count, face_slot, face_count, node_coord, coarse_inverse):
     axes = ("group", "member")
     packed = 12 * DEV + LN
-    modes, pay0 = call(
+    raw = (load, dof_map, dof_sign, live_count, face_slot, face_count, coarse_inverse)
+    modes, pay0, *raw = call(
         coarse_kernel,
-        (sds((2, 8, ND)), sds((DEV, LN))),
-        {0: HB, 1: HB},
-        load, node_coord.transpose(0, 2, 1, 3),
-        scratch=[
-            pltpu.VMEM(load.shape, load.dtype), pltpu.VMEM((1, 3, 2, 256), node_coord.dtype),
-            pltpu.SemaphoreType.DMA((2,)),
-        ],
+        (sds((2, 8, ND)), sds((DEV, LN))) + tuple(sds(r.shape, r.dtype) for r in raw),
+        {i: HB for i in range(8)},
+        load, node_coord.transpose(0, 2, 1, 3), *raw[1:],
+        scratch=[pltpu.VMEM((1, 3, 2, 256), node_coord.dtype), pltpu.SemaphoreType.DMA((8,))],
     )
 
     def exchange(pay):
         return lax.all_to_all(pay, axes, 0, 0, tiled=True)
 
     recv0 = exchange(pay0)
-    raw = (load, dof_map, dof_sign, live_count, face_slot, face_count, coarse_inverse)
     tt, qt, own, aux, to_sib, to_far, to_g1, to_g2, diag = call(
         tables_kernel,
         (
             sds((2, ND, 256), BF), pltpu.HBM((2, ND, ND), BF), pltpu.HBM((2, 16, ND), F32), sds((8, ND)),
             sds((8, packed)), sds((8, packed)), sds((16, packed)), sds((16, packed)), sds((2 * NCH, LN, LN)),
         ),
-        {i: HB for i in range(1, 9)},
+        {8: HB},
         modes, *raw, factor,
-        scratch=[pltpu.VMEM(r.shape, r.dtype) for r in raw]
-        + [pltpu.VMEM((2, 16, ND), F32), pltpu.VMEM((2, ND, ND), BF), pltpu.SemaphoreType.DMA((10,)), pltpu.SemaphoreType.DMA((2 * NCH,))],
+        scratch=[
+            pltpu.VMEM((2, 16, ND), F32), pltpu.VMEM((2, ND, ND), BF),
+            pltpu.SemaphoreType.DMA((3,)), pltpu.SemaphoreType.DMA((2 * NCH,)),
+        ],
         hbm_outs=(1, 2),
     )
 
@@ -701,14 +703,17 @@
         mib=24,
     )
     near = jnp.concatenate([from_sib, from_far, from_g1, from_g2], axis=0)
-    st_s, o_s, hs_s, row_s = sds((12, ND)), sds((2, 256)), sds((24, DEV)), sds((8, LN))
-
-    def gather(row, o):
-        (pay,) = call(pay_kernel, (sds((DEV, LN)),), {}, row, lax.ppermute(row, "member", swap), o)
+    st_s, o_s, hs_s = sds((12, ND)), sds((2, 256)), sds((24, DEV))
+
+    def gather(count, st, o):
+        other = lax.ppermute(o, "member", swap)
+        (row,) = call(make_coef(count), (sds((8, LN)),), {}, st, ar, aux)
+        (pay,) = call(pay_kernel, (sds((DEV, LN)),), {}, row, other, o)
         return exchange(pay)
 
-    ar, table, st, o, row = call(
-        begin_kernel, (sds((2, 40, ND)), sds((64, 12 * DEV)), st_s, o_s, row_s),
+    ar, table, st, o = call(
+        begin_kernel,
+        (sds((2, 40, ND)), sds((64, 12 * DEV)), st_s, o_s),
         {3: HB, 4: HB},
         recv0, tt, aux, inv, own, to_g1, near,
         scratch=[
@@ -716,16 +721,16 @@
             pltpu.SemaphoreType.DMA((1,)), pltpu.SemaphoreType.DMA((2 * NCH,)),
         ],
     )
-    st, o, row = call(first_kernel, (st_s, o_s, row_s), {}, gather(row, o), st, o, inv, tt, ar, table, aux)
+    st, o = call(first_kernel, (st_s, o_s), {}, gather(0, st, o), st, o, inv, tt, ar, table, aux)
     hs = jnp.zeros((24, DEV), F32)
     for it in range(ITERS - 1):
-        st, o, hs, row = call(
-            make_step(it), (st_s, o_s, hs_s, row_s), {},
-            gather(row, o), st, o, hs, inv, tt, ar, table, aux,
+        st, o, hs = call(
+            make_step(it), (st_s, o_s, hs_s), {},
+            gather(4 if it else 2, st, o), st, o, hs, inv, tt, ar, table, aux,
         )
     lam, proj = call(
         last_kernel, (sds((2, ND)), sds((2, ND))), {},
-        gather(row, o), st, o, hs, tt, ar, table, aux, qt,
+        gather(4, st, o), st, o, hs, tt, ar, table, aux, qt,
     )
     return lam[None], proj[None]
 

time: 132 us -> 132 us (level)
    pallas_call x12 -> x16, Pallas kernels: 21 us -> 21.8 us  [call(): pl.pallas_call(kernel, out_shape=outs, in_specs=[specs.get(i, VM) for i i...]
  transfers between devices with their start and end apart: 9 -> 9, of which waited for: 5 -> 5; matrix products, arithmetic and copies ran while one was open for 0% -> 0% of each run, Pallas kernels for 5% -> 6%
where the time goes in v4:
time: 132 us
  blocking collectives  74.2 us (56%)
  starting transfers between devices  26.9 us (20%)
  Pallas kernels  21.8 us (17%)
  waiting for transfers between devices  8.35 us (6%)
    all_to_all x4, blocking collectives, exchange(): return lax.all_to_all(pay, axes, 0, 0, tiled=True)  74.2 us
    pallas_call x16, Pallas kernels, call(): pl.pallas_call(kernel, out_shape=outs, in_specs=[specs.get(i, VM) for i i...  21.8 us
    all_to_all x1, starting transfers between devices, exchange(): return lax.all_to_all(pay, axes, 0, 0, tiled=True)  15.5 us
    all_to_all x1, waiting for transfers between devices, exchange(): return lax.all_to_all(pay, axes, 0, 0, tiled=True)  5.94 us
    ppermute x4, starting transfers between devices, gather(): other = lax.ppermute(o, 'member', swap)  4.07 us
    ppermute x1, starting transfers between devices, shards(): from_far = lax.ppermute(to_far, 'member', cross)  3.2 us
  transfers between devices with their start and end apart: 9, of which 5 were waited for; matrix products, arithmetic and copies ran while one was open for 0% of the time, Pallas kernels for 6%

profile of v4, /device:TPU:1, one launch (start us, length us, event | category | flops | bytes accessed | tf_op | source)
XLA Modules:
  0.0 132.1 jit_solution(17346265049125193995)
XLA Ops:
  0.6 1.8 %shard_map.104 = (f32[2,8,768]{2,1,0:T(8,128)S(1)}, f32[256,128]{1,0:T(8,128)}, f32[1,2,768]{2,1,0:T(2,128)S(1)}, s32[1,2,768]{2,1,0:T(2,128)S(1)}, s32[1,2,768]...) custom-call(f32[1,2,768]{2,1,0:T(2,128)} %load_hbm.1, ...), custom_call_target="tpu_custom_call" | custom-call | tf_op jit(solution)/shard_map/pallas_call | solution.py:641
  2.4 4.4 %shard_map.105 = (bf16[2,768,256]{2,1,0:T(8,128)(2,1)S(1)}, bf16[2,768,768]{2,1,0:T(8,128)(2,1)}, f32[2,16,768]{2,1,0:T(8,128)}, f32[8,768]{1,0:T(8,128)S(1)}, f...) custom-call(f32[2,8,768]{2,1,0:T(8,128)S(1)} %get-tuple-element.35.m, ...), custom_call_target="tpu_custom_call" | custom-call | tf_op jit(solution)/shard_map/pallas_call | solution.py:641
  6.8 2.1 %collective-permute-start.2 = (f32[16,3200]{1,0:T(8,128)S(1)}, f32[16,3200]{1,0:T(8,128)S(1)}, u32[]{:S(2)}, u32[]{:S(2)}) collective-permute-start(f32[16,3200]{1,0:T(8,128)S(1)} %get-tuple-element.47.mine_ref), channel_id=1, source_target_pairs={{0,16},{16,0},{32,48},{48,32},{64,80},{80,64},{96,112},{112,96},{1... | collective-permute-start | bytes 614408 | tf_op jit(solution)/shard_map/ppermute | solution.py:687
  8.9 0.7 collective-permute-start.3
  9.6 1.3 collective-permute-start
  10.9 3.2 %collective-permute-start.1 = (f32[8,3200]{1,0:T(8,128)S(1)}, f32[8,3200]{1,0:T(8,128)S(1)}, u32[]{:S(2)}, u32[]{:S(2)}) collective-permute-start(f32[8,3200]{1,0:T(8,128)S(1)} %get-tuple-element.49), channel_id=1, source_target_pairs={{1,2},{2,1},{3,4},{4,3},{5,6},{6,5},{7,8},{8,7},{9,10},{10,9},{11,... | collective-permute-start | bytes 307208 | tf_op jit(solution)/shard_map/ppermute | solution.py:689
  14.1 15.5 %all-to-all-start = ((f32[256,1,128]{2,1,0:T(1,128)}), f32[256,1,128]{2,1,0:T(1,128)S(1)}, u32[]{:S(2)}, u32[]{:S(2)}) async-start(f32[256,1,128]{2,1,0:T(1,128)} %bitcast.2), calls=%async_computation | async-start | bytes 262144 | tf_op jit(solution)/shard_map/all_to_all | solution.py:667
  29.7 6.8 %shard_map.106.inv_hbm.inv_ref = f32[2,768,768]{2,1,0:T(8,128)} custom-call(f32[1,2,768,768]{3,2,1,0:T(8,128)} %l_hbm.3, f32[12,128,128]{2,1,0:T(8,128)S(1)} %get-tuple-element.45.diag_ref), custom_call_target="tpu_custom_call" | custom-call | flops 20000000000 | bytes 1048576 | tf_op jit(solution)/shard_map/pallas_call | solution.py:641
  36.6 5.9 %all-to-all-done = f32[256,1,128]{2,1,0:T(1,128)S(1)} async-done(((f32[256,1,128]{2,1,0:T(1,128)}), f32[256,1,128]{2,1,0:T(1,128)S(1)}, u32[]{:S(2)}, u32[]{:S(2)}) %all-to-all-start) | async-done | bytes 131104 | tf_op jit(solution)/shard_map/all_to_all | solution.py:667
  42.5 2.9 %shard_map.107 = (f32[2,40,768]{2,1,0:T(8,128)S(1)}, f32[64,3072]{1,0:T(8,128)S(1)}, f32[12,768]{1,0:T(8,128)S(1)}, f32[2,256]{1,0:T(2,128)S(1)}) custom-call(f32[256,128]{1,0:T(8,128)S(1)} %bitcast.23, bf16[2,768,256]{2,1,0:T(8,128)(2,1)S(1)} %get-tuple-element.43.tt_ref, f32[8,768]{1,0:T(8,128)S(1)} %get-tuple-element.44.aux_ref, ...), custom_call_target="tpu_custom_call" | custom-call | tf_op jit(solution)/shard_map/pallas_call | solution.py:641
  45.5 1.2 collective-permute-start.4
  46.6 0.2 shard_map.108.row_ref
  46.9 0.6 collective-permute-done.4.sib_ref
  47.5 0.1 shard_map.109
  47.6 19.9 %all_to_all.55 = f32[256,1,128]{2,1,0:T(1,128)S(1)} all-to-all(f32[256,1,128]{2,1,0:T(1,128)S(1)} %bitcast.28), channel_id=1, replica_groups=mesh['group'=16,'member'=16] {'group','member'}, dimensions={0} | all-to-all | bytes 262144 | tf_op jit(solution)/shard_map/all_to_all | solution.py:667
  67.5 1.0 shard_map.110
  68.5 1.0 collective-permute-start.5
  69.5 0.2 shard_map.111.row_ref
  69.7 0.6 collective-permute-done.5.sib_ref
  70.3 0.1 shard_map.112
  70.4 18.1 %all_to_all.56 = f32[256,1,128]{2,1,0:T(1,128)S(1)} all-to-all(f32[256,1,128]{2,1,0:T(1,128)S(1)} %bitcast.29), channel_id=1, replica_groups=mesh['group'=16,'member'=16] {'group','member'}, dimensions={0} | all-to-all | bytes 262144 | tf_op jit(solution)/shard_map/all_to_all | solution.py:667
  88.5 1.0 shard_map.113
  89.6 1.0 collective-permute-start.6
  90.5 0.2 shard_map.114.row_ref
  90.8 0.6 collective-permute-done.6.sib_ref
  91.4 18.1 %all_to_all.57 = f32[256,1,128]{2,1,0:T(1,128)S(1)} all-to-all(f32[256,1,128]{2,1,0:T(1,128)S(1)} %bitcast.30), channel_id=1, replica_groups=mesh['group'=16,'member'=16] {'group','member'}, dimensions={0} | all-to-all | bytes 262144 | tf_op jit(solution)/shard_map/all_to_all | solution.py:667
  109.5 1.1 shard_map.116
  110.6 1.0 collective-permute-start.7
  111.6 0.2 shard_map.117.row_ref
  111.8 0.6 collective-permute-done.7.sib_ref
  112.5 18.1 %all_to_all.58 = f32[256,1,128]{2,1,0:T(1,128)S(1)} all-to-all(f32[256,1,128]{2,1,0:T(1,128)S(1)} %bitcast.31), channel_id=1, replica_groups=mesh['group'=16,'member'=16] {'group','member'}, dimensions={0} | all-to-all | bytes 262144 | tf_op jit(solution)/shard_map/all_to_all | solution.py:667
  130.5 1.5 %shard_map.119 = (f32[2,768]{1,0:T(2,128)}, f32[2,768]{1,0:T(2,128)}) custom-call(f32[256,128]{1,0:T(8,128)S(1)} %bitcast.24, f32[12,768]{1,0:T(8,128)S(1)} %get-tuple-element.60.st_ref, f32[2,256]{1,0:T(2,128)S(1)} %get-tuple-element.61.o_ref, f32[24,256]{1,0:T(8,128)S(1)} %get-tuple-element.62.hs_ref, bf16[2,768,256]{2,1,0:T(8,128)(2,1)S(1)} %get-tuple-element.43.tt_ref, ...), custom_call_target="tpu_custom_call" | custom-call | tf_op jit(solution)/shard_map/pallas_call | solution.py:641
  (12 shorter events, 0.3 us)
Async XLA Ops:
  6.8 29.7 %collective-permute-start.2 = (f32[16,3200]{1,0:T(8,128)S(1)}, f32[16,3200]{1,0:T(8,128)S(1)}, u32[]{:S(2)}, u32[]{:S(2)}) collective-permute-start(f32[16,3200]{1,0:T(8,128)S(1)} %get-tuple-element.47.mine_ref), channel_id=1, source_target_pairs={{0,16},{16,0},{32,48},{48,32},{64,80},{80,64},{96,112},{112,96},{1... | collective-permute-start | bytes 614408 | tf_op jit(solution)/shard_map/ppermute | solution.py:687
  8.9 27.6 %collective-permute-start.3 = (f32[16,3200]{1,0:T(8,128)S(1)}, f32[16,3200]{1,0:T(8,128)S(1)}, u32[]{:S(2)}, u32[]{:S(2)}) collective-permute-start(f32[16,3200]{1,0:T(8,128)S(1)} %get-tuple-element.50), channel_id=1, source_target_pairs={{16,32},{32,16},{48,64},{64,48},{80,96},{96,80},{112,128},{128,112... | collective-permute-start | bytes 614408 | tf_op jit(solution)/shard_map/ppermute | solution.py:688
  9.6 26.9 %collective-permute-start = (f32[8,3200]{1,0:T(8,128)S(1)}, f32[8,3200]{1,0:T(8,128)S(1)}, u32[]{:S(2)}, u32[]{:S(2)}) collective-permute-start(f32[8,3200]{1,0:T(8,128)S(1)} %get-tuple-element.48), channel_id=1, source_target_pairs={{0,1},{1,0},{2,3},{3,2},{4,5},{5,4},{6,7},{7,6},{8,9},{9,8},{10,11... | collective-permute-start | bytes 307208 | tf_op jit(solution)/shard_map/ppermute | solution.py:690
  10.9 25.6 %collective-permute-start.1 = (f32[8,3200]{1,0:T(8,128)S(1)}, f32[8,3200]{1,0:T(8,128)S(1)}, u32[]{:S(2)}, u32[]{:S(2)}) collective-permute-start(f32[8,3200]{1,0:T(8,128)S(1)} %get-tuple-element.49), channel_id=1, source_target_pairs={{1,2},{2,1},{3,4},{4,3},{5,6},{6,5},{7,8},{8,7},{9,10},{10,9},{11,... | collective-permute-start | bytes 307208 | tf_op jit(solution)/shard_map/ppermute | solution.py:689
  14.1 28.4 %all-to-all-start = ((f32[256,1,128]{2,1,0:T(1,128)}), f32[256,1,128]{2,1,0:T(1,128)S(1)}, u32[]{:S(2)}, u32[]{:S(2)}) async-start(f32[256,1,128]{2,1,0:T(1,128)} %bitcast.2), calls=%async_computation | async-start | bytes 262144 | tf_op jit(solution)/shard_map/all_to_all | solution.py:667
  42.5 25.0 %copy-start = (f32[2,768,768]{2,1,0:T(8,128)S(1)}, f32[2,768,768]{2,1,0:T(8,128)}, u32[]{:S(2)}) copy-start(f32[2,768,768]{2,1,0:T(8,128)} %shard_map.106.inv_hbm.inv_ref) | copy-start | bytes 14155780
  45.5 2.0 %collective-permute-start.4 = (f32[2,256]{1,0:T(2,128)S(1)}, f32[2,256]{1,0:T(2,128)S(1)}, u32[]{:S(2)}, u32[]{:S(2)}) collective-permute-start(f32[2,256]{1,0:T(2,128)S(1)} %get-tuple-element.53.o_ref), channel_id=1, source_target_pairs={{0,1},{1,0},{2,3},{3,2},{4,5},{5,4},{6,7},{7,6},{8,9},{9,8},{10,11... | collective-permute-start | bytes 6152 | tf_op jit(solution)/shard_map/ppermute | solution.py:709
  68.5 1.8 %collective-permute-start.5 = (f32[2,256]{1,0:T(2,128)S(1)}, f32[2,256]{1,0:T(2,128)S(1)}, u32[]{:S(2)}, u32[]{:S(2)}) collective-permute-start(f32[2,256]{1,0:T(2,128)S(1)} %get-tuple-element.56.o_ref), channel_id=1, source_target_pairs={{0,1},{1,0},{2,3},{3,2},{4,5},{5,4},{6,7},{7,6},{8,9},{9,8},{10,11... | collective-permute-start | bytes 6152 | tf_op jit(solution)/shard_map/ppermute | solution.py:709
  89.5 41.0 %copy-start.1 = (bf16[2,768,768]{2,1,0:T(8,128)(2,1)S(1)}, bf16[2,768,768]{2,1,0:T(8,128)(2,1)}, u32[]{:S(2)}) copy-start(bf16[2,768,768]{2,1,0:T(8,128)(2,1)} %get-tuple-element.63.qt_ref) | copy-start | bytes 7077892
  89.6 1.8 %collective-permute-start.6 = (f32[2,256]{1,0:T(2,128)S(1)}, f32[2,256]{1,0:T(2,128)S(1)}, u32[]{:S(2)}, u32[]{:S(2)}) collective-permute-start(f32[2,256]{1,0:T(2,128)S(1)} %get-tuple-element.58.o_ref), channel_id=1, source_target_pairs={{0,1},{1,0},{2,3},{3,2},{4,5},{5,4},{6,7},{7,6},{8,9},{9,8},{10,11... | collective-permute-start | bytes 6152 | tf_op jit(solution)/shard_map/ppermute | solution.py:709
  110.6 1.8 %collective-permute-start.7 = (f32[2,256]{1,0:T(2,128)S(1)}, f32[2,256]{1,0:T(2,128)S(1)}, u32[]{:S(2)}, u32[]{:S(2)}) collective-permute-start(f32[2,256]{1,0:T(2,128)S(1)} %get-tuple-element.61.o_ref), channel_id=1, source_target_pairs={{0,1},{1,0},{2,3},{3,2},{4,5},{5,4},{6,7},{7,6},{8,9},{9,8},{10,11... | collective-permute-start | bytes 6152 | tf_op jit(solution)/shard_map/ppermute | solution.py:709
